TPU v7x, 128 devices: a whole 4x4x4 slice. The times are simulated.
128 devices in a mesh: wide: 32 (over x, z, y_lo), narrow: 4 (over y_hi, core).
Axes of the slice: x: 4, y: 4 (y_hi: 2, y_lo: 2; y = y_hi * 2 + y_lo), z: 4, core: 2. Of those that a mesh axis runs over, the one named last changes fastest.
Arguments:
- fine_in: bfloat16 [16, 64, 256, 512], P(None, None, 'wide', 'narrow'), may hold values from -6 to 6
- coarse_in: bfloat16 [64, 64, 64, 128], P(None, 'wide', 'narrow'), may hold values from -6 to 6
- w_fine1: bfloat16 [16, 16, 3, 3, 3], replicated, may hold values from -0.3125 to 0.3125
- b_fine1: float32 [16], replicated, may hold values from -3 to 3
- w_fine2: bfloat16 [16, 16, 3, 3, 3], replicated, may hold values from -0.3125 to 0.3125
- b_fine2: float32 [16], replicated, may hold values from -3 to 3
- w_coarse1: bfloat16 [64, 80, 3, 3, 3], replicated, may hold values from -0.125 to 0.125
- b_coarse1: float32 [64], replicated, may hold values from -3 to 3
- w_coarse2: bfloat16 [64, 64, 3, 3, 3], replicated, may hold values from -0.15625 to 0.15625
- b_coarse2: float32 [64], replicated, may hold values from -3 to 3
- w_proj: bfloat16 [16, 64], replicated, may hold values from -0.75 to 0.75
Outputs:
- fine_out: bfloat16 [16, 64, 256, 512], P(None, None, 'wide', 'narrow')
- coarse_out: bfloat16 [64, 64, 64, 128], P(None, 'wide', 'narrow')
All inputs are finite; a program needn't handle non-finite values.
Results may differ from a plain program's by a relative error of at most 0.0075.
Values may be sent and summed in bfloat16 or wider, within the bound.
No kernel may reach another device: no remote copies, remote signals or barrier semaphores. Data moves between devices by JAX's collectives and lax.ppermute only.
A program may use at most 192 MiB of HBM per device.

v0:
```python
import functools

import jax
import jax.numpy as jnp
from jax import lax
from jax.experimental import pallas as pl
from jax.experimental.pallas import tpu as pltpu
from jax.sharding import PartitionSpec as P


BF = jnp.bfloat16
F32 = jnp.float32
INTERPRET = False


def iota(shape, axis):
    return lax.broadcasted_iota(jnp.int32, shape, axis)


def onehot(mask):
    return jnp.where(mask, 1.0, 0.0).astype(BF)


def mm(a, b):
    return jnp.dot(a, b, preferred_element_type=F32)


def vm(n):
    return [pl.BlockSpec(memory_space=pltpu.VMEM)] * n


def outer_columns(rows, first_z):
    shape = (rows.shape[1], 128)
    r, lane = iota(shape, 0), iota(shape, 1)
    z, x = first_z + r // 128, r % 128
    return mm(rows, onehot(((x == 0) & (lane == z)) | ((x == 127) & (lane == z + 64))))


def prep_body(x_ref, t_ref, cols_ref, acc_ref):
    step = pl.program_id(0)
    zb = t_ref.shape[0]
    r, k = iota((128, 128), 0), iota((128, 128), 1)
    perm = onehot((r % 16) * 8 + r // 16 == k)
    rows = []
    for i in range(0, zb, 2):
        pair = jnp.concatenate([x_ref[:, step * zb + i + j].reshape(128, 128) for j in range(2)], axis=1)
        out = mm(perm, pair).astype(BF)
        for j in range(2):
            t_ref[i + j] = out[:, j * 128 : j * 128 + 128]
        rows.append(out)
    part = outer_columns(jnp.concatenate(rows, axis=1), step * zb)

    @pl.when(step == 0)
    def _():
        acc_ref[...] = part

    @pl.when(step > 0)
    def _():
        acc_ref[...] += part

    cols_ref[...] = acc_ref[...].astype(BF)


def prep(x):
    zb = 8
    return pl.pallas_call(
        prep_body,
        grid=(64 // zb,),
        in_specs=[pl.BlockSpec((16, 64, 8, 128), lambda i: (0, 0, 0, 0))],
        out_specs=[
            pl.BlockSpec((zb, 128, 128), lambda i: (i, 0, 0)),
            pl.BlockSpec((128, 128), lambda i: (0, 0)),
        ],
        out_shape=[jax.ShapeDtypeStruct((64, 128, 128), BF), jax.ShapeDtypeStruct((128, 128), BF)],
        scratch_shapes=[pltpu.VMEM((128, 128), F32)],
        interpret=INTERPRET,
        name="prep",
    )(x)


def cprep_body(x_ref, o_ref):
    r, k = iota((256, 256), 0), iota((256, 256), 1)
    perm = onehot((r % 16) * 16 + r // 16 == k)
    for g in range(4):
        pair = jnp.concatenate(
            [x_ref[g * 16 : g * 16 + 16, z].reshape(256, 128) for z in range(2)], axis=1
        )
        out = mm(perm, pair).astype(BF)
        for z in range(2):
            for y in range(16):
                o_ref[z, y, g * 16 : g * 16 + 16, :] = out[y * 16 : y * 16 + 16, z * 128 : z * 128 + 128]


def cprep(x):
    return pl.pallas_call(
        cprep_body,
        in_specs=vm(1),
        out_specs=vm(1)[0],
        out_shape=jax.ShapeDtypeStruct((2, 16, 64, 128), BF),
        interpret=INTERPRET,
        name="cprep",
    )(x)


def kept(ok, v):
    return jnp.where(ok, v, jnp.zeros((), BF))


def stage(z, at_ref, x_ref, top_ref, bot_ref, tl_ref, tr_ref, s_ref):
    rows = pl.ds(pl.multiple_of(z * 16, 16), 16)
    top = kept(at_ref[3] > 0, top_ref[rows, :])
    bot = kept(at_ref[3] < 31, bot_ref[rows, :])
    v = jnp.concatenate([top, x_ref[z], bot], axis=0)
    lane = iota((160, 128), 1)
    left = jnp.where(lane == 0, pltpu.roll(tl_ref[...], lax.rem(192 - z, 128), 1), pltpu.roll(v, 1, 1))
    right = jnp.where(lane == 127, pltpu.roll(tr_ref[...], 127 - z, 1), pltpu.roll(v, 127, 1))
    base = pl.multiple_of((z + 1) * 512, 512)
    s_ref[pl.ds(base, 160), :] = left
    s_ref[pl.ds(base + 160, 160), :] = v
    s_ref[pl.ds(base + 320, 160), :] = right


def conv_pair(z, w_ref, s_ref):
    base = pl.multiple_of(z * 512, 512)
    rhs = jnp.concatenate([s_ref[pl.ds(base, 1536), :], s_ref[pl.ds(base + 512, 1536), :]], axis=1)
    return mm(w_ref[...], rhs)


def bias_rows(b_ref, by_channel):
    r, k = iota((128, 16), 0), iota((128, 16), 1)
    mask = (r // 8 if by_channel else r % 16) == k
    return jnp.sum(jnp.where(mask, b_ref[...], 0.0), axis=1, keepdims=True)


def fine_setup(at_ref, k_ref, top_ref, bot_ref, cl_ref, cr_ref, w_ref, w0_ref, s_ref, tl_ref, tr_ref, by_channel):
    w0_ref[...] = jnp.zeros((16, 1536), F32)
    for t in range(27):
        dz, dy, dx = t // 9, t // 3 % 3, t % 3
        at = dz * 512 + dx * 160 + dy * 16
        w0_ref[:, at : at + 16] = k_ref[t].astype(F32)
    w0 = w0_ref[...]
    for y in range(8):
        w_ref[y * 16 : y * 16 + 16, :] = (pltpu.roll(w0, y * 16, 1) if y else w0).astype(BF)
    if by_channel:
        r, k = iota((128, 128), 0), iota((128, 128), 1)
        w_ref[...] = mm(onehot((r % 8) * 16 + r // 8 == k), w_ref[...]).astype(BF)
    n, w = at_ref[2], at_ref[3]
    for ref, edge, col, ok in ((tl_ref, 1024, cl_ref, n > 0), (tr_ref, 1040, cr_ref, n < 3)):
        ref[0:16, :] = kept(ok & (w > 0), top_ref[edge : edge + 16, :])
        ref[16:144, :] = kept(ok, col[0:128, :])
        ref[144:160, :] = kept(ok & (w < 31), bot_ref[edge : edge + 16, :])
    s_ref[0:512, :] = jnp.zeros((512, 128), BF)
    s_ref[65 * 512 : 66 * 512, :] = jnp.zeros((512, 128), BF)
    if not by_channel:
        for z in range(1, 65):
            s_ref[z * 512 + 480 : z * 512 + 512, :] = jnp.zeros((32, 128), BF)


def run_conv(stage_fn, finish, w_ref, s_ref):
    for z in range(5):
        stage_fn(z)

    def step(i, _):
        first = conv_pair(4 * i, w_ref, s_ref)
        second = conv_pair(4 * i + 2, w_ref, s_ref)
        for k in range(5, 9):
            stage_fn(4 * i + k)
        finish(2 * i, first)
        finish(2 * i + 1, second)
        return 0

    lax.fori_loop(0, 14, step, 0)
    first = conv_pair(56, w_ref, s_ref)
    second = conv_pair(58, w_ref, s_ref)
    for k in range(61, 64):
        stage_fn(k)
    finish(28, first)
    finish(29, second)
    first = conv_pair(60, w_ref, s_ref)
    second = conv_pair(62, w_ref, s_ref)
    finish(30, first)
    finish(31, second)


def fine1_body(at_ref, x_ref, top_ref, bot_ref, cl_ref, cr_ref, k_ref, b_ref, h_ref, p_ref, cols_ref, s_ref, w_ref, w0_ref, tl_ref, tr_ref, acc_ref):
    fine_setup(at_ref, k_ref, top_ref, bot_ref, cl_ref, cr_ref, w_ref, w0_ref, s_ref, tl_ref, tr_ref, False)
    bias = bias_rows(b_ref, False)

    def finish(i, out):
        h = jnp.maximum(out + bias, 0.0).astype(BF)
        parts = []
        for k in range(2):
            hz = h[:, k * 128 : (k + 1) * 128]
            h_ref[2 * i + k] = hz
            f = hz.astype(F32)
            for half in range(2):
                r = f[half * 64 : half * 64 + 64]
                parts.append((r[0:16] + r[16:32]) + (r[32:48] + r[48:64]))
        hi = [p.astype(BF) for p in parts]
        lo = [(p - q.astype(F32)).astype(BF) for p, q in zip(parts, hi)]
        acc_ref[pl.ds(pl.multiple_of(i * 16, 16), 16), :] = jnp.concatenate(hi + lo, axis=1)

    run_conv(lambda z: stage(z, at_ref, x_ref, top_ref, bot_ref, tl_ref, tr_ref, s_ref), finish, w_ref, s_ref)
    r, lane = iota((1024, 128), 0) % 512, iota((1024, 128), 1)
    pick = jnp.where((r // 128) * 32 + (r % 128) // 4 == lane, 0.0625, 0.0).astype(BF)
    pooled = mm(acc_ref[...], pick).astype(BF)
    nothing = jnp.zeros((16, 128), BF)
    a, b = at_ref[0], at_ref[1]
    for to in range(4):
        goes = (a == to) | ((a == to - 1) & (b == 7)) | ((a == to + 1) & (b == 0))
        sent = kept(goes, pooled)
        for slab in range(32):
            for j in range(3):
                at = slab + j - 1
                block = sent[at * 16 : at * 16 + 16] if 0 <= at < 32 else nothing
                p_ref[slab, to, j * 16 : j * 16 + 16, :] = block
    total = jnp.zeros((128, 128), F32)
    for g in range(8):
        total = total + outer_columns(jnp.concatenate([h_ref[g * 8 + k] for k in range(8)], axis=1), g * 8)
    cols_ref[...] = total.astype(BF)


def fine_scratch():
    return [
        pltpu.VMEM((66 * 512, 128), BF),
        pltpu.VMEM((128, 1536), BF),
        pltpu.VMEM((16, 1536), F32),
        pltpu.VMEM((160, 128), BF),
        pltpu.VMEM((160, 128), BF),
    ]


def fine1(at, x, top, bot, cl, cr, k, b):
    return pl.pallas_call(
        fine1_body,
        in_specs=[pl.BlockSpec(memory_space=pltpu.SMEM)] + vm(7),
        out_specs=vm(3),
        out_shape=[
            jax.ShapeDtypeStruct((64, 128, 128), BF),
            jax.ShapeDtypeStruct((32, 4, 48, 128), BF),
            jax.ShapeDtypeStruct((128, 128), BF),
        ],
        scratch_shapes=fine_scratch() + [pltpu.VMEM((512, 1024), BF)],
        interpret=INTERPRET,
        name="fine1",
    )(at, x, top, bot, cl, cr, k, b)


def fine2_body(at_ref, x_ref, top_ref, bot_ref, cl_ref, cr_ref, k_ref, b_ref, c_ref, o_ref, s_ref, w_ref, w0_ref, tl_ref, tr_ref):
    fine_setup(at_ref, k_ref, top_ref, bot_ref, cl_ref, cr_ref, w_ref, w0_ref, s_ref, tl_ref, tr_ref, True)
    bias = bias_rows(b_ref, True)
    r, lane = iota((128, 512), 0), iota((128, 512), 1)
    up = onehot((lane // 128) * 32 + (lane % 128) // 4 == r)
    for g in range(4):
        e = mm(c_ref[g * 8 : g * 8 + 8].reshape(128, 128), up).astype(BF)
        for p in range(8):
            for q in range(4):
                z = 2 * (g * 8 + p) + q // 2
                row = (z + 1) * 512 + 480 + (q % 2) * 16
                s_ref[row : row + 16, :] = e[p * 16 : p * 16 + 16, q * 128 : q * 128 + 128]
    rr, kk = iota((128, 32), 0), iota((128, 32), 1)
    w_ref[:, 992:1024] = onehot((kk % 16 == rr // 8) & (kk // 16 == (rr % 8) // 4))

    def finish(i, out):
        v = out + bias
        for k in range(2):
            o_ref[:, 2 * i + k] = v[:, k * 128 : (k + 1) * 128].reshape(16, 8, 128).astype(BF)

    run_conv(lambda z: stage(z, at_ref, x_ref, top_ref, bot_ref, tl_ref, tr_ref, s_ref), finish, w_ref, s_ref)


def fine2(at, x, top, bot, cl, cr, k, b, c):
    def whole(*shape):
        return pl.BlockSpec(shape, lambda i, at: (0,) * len(shape))

    return pl.pallas_call(
        fine2_body,
        grid_spec=pltpu.PrefetchScalarGridSpec(
            num_scalar_prefetch=1,
            grid=(1,),
            in_specs=[
                whole(64, 128, 128),
                whole(1056, 128),
                whole(1056, 128),
                whole(128, 128),
                whole(128, 128),
                whole(27, 16, 16),
                whole(1, 16),
                pl.BlockSpec((32, 1, 16, 128), lambda i, at: (0, at[0], 0, 0)),
            ],
            out_specs=whole(16, 64, 8, 128),
            scratch_shapes=fine_scratch(),
        ),
        out_shape=jax.ShapeDtypeStruct((16, 64, 8, 128), BF),
        interpret=INTERPRET,
        name="fine2",
    )(at, x, top, bot, cl, cr, k, b, c)


def spread_x(v):
    lane = iota(v.shape, 1)
    left = jnp.where(lane == 0, jnp.zeros((), BF), pltpu.roll(v, 1, 1))
    right = jnp.where(lane == 127, jnp.zeros((), BF), pltpu.roll(v, 127, 1))
    return jnp.concatenate([left, v, right], axis=0)


def window(s_ref, z, y, rows, per_z):
    both = []
    for k in range(2):
        parts = [
            s_ref[pl.ds(pl.multiple_of((z + dz) * per_z + (y + k) * rows, 16), 3 * rows), :] for dz in range(3)
        ]
        both.append(jnp.concatenate(parts, axis=0))
    return jnp.concatenate(both, axis=1)


def conv1a_body(masked, at_ref, first_ref, second_ref, k_ref, b_ref, o_ref, s_ref, w_ref):
    swap = at_ref[4] == 1
    reaches = at_ref[5] == 1
    for t in range(27):
        w_ref[:, t * 64 : t * 64 + 64] = k_ref[t][:, 0:64]

    def fill(y, _):
        for zi in range(2):
            a, b = first_ref[zi, y], second_ref[zi, y]
            if masked:
                a = kept(reaches, a)
            for at, v in ((zi, jnp.where(swap, b, a)), (zi + 2, jnp.where(swap, a, b))):
                s_ref[pl.ds(pl.multiple_of(at * 3840 + y * 192, 64), 192), :] = spread_x(v)
        return 0

    lax.fori_loop(0, 20, fill, 0)
    bias = b_ref[...]

    def step(i, _):
        outs = [
            mm(w_ref[...], window(s_ref, zo, 6 * i + 2 * k, 192, 3840)) + bias for zo in range(2) for k in range(3)
        ]
        for j in range(6):
            o_ref[j // 3 * 9 + 3 * i + j % 3] = outs[j]
        return 0

    lax.fori_loop(0, 3, step, 0)


def conv1a(at, first, second, k, b, name):
    return pl.pallas_call(
        functools.partial(conv1a_body, name == "distant"),
        in_specs=[pl.BlockSpec(memory_space=pltpu.SMEM)] + vm(4),
        out_specs=vm(1)[0],
        out_shape=jax.ShapeDtypeStruct((18, 64, 256), F32),
        scratch_shapes=[pltpu.VMEM((4 * 20 * 192, 128), BF), pltpu.VMEM((64, 1728), BF)],
        interpret=INTERPRET,
    )(at, first, second, k, b)


def coarse_body(at_ref, main_ref, lo_ref, hi_ref, near_ref, far_ref, k1_ref, k2_ref, b_ref, proj_ref, out_ref, ctx_ref, sp_ref, sm_ref, w1_ref, w2_ref, co_ref, ct_ref):
    n, w = at_ref[2], at_ref[3]
    odd = at_ref[4] == 1
    for t in range(27):
        w1_ref[:, t * 16 : t * 16 + 16] = k1_ref[t][:, 64:80]
        w2_ref[:, t * 64 : t * 64 + 64] = k2_ref[t]
    r, c = iota((512, 512), 0), iota((512, 512), 1)
    order = onehot((r % 128 // 32 == c // 128) & (r // 128 == c % 128 // 32) & (r % 32 == c % 32))
    for wb in range(10):
        if wb == 0:
            blocks = [jnp.where(n > 0, lo_ref[0, k], jnp.zeros((48, 128), BF)) for k in range(4)]
        elif wb == 9:
            blocks = [jnp.where(n < 3, hi_ref[0, k], jnp.zeros((48, 128), BF)) for k in range(4)]
        else:
            blocks = [main_ref[wb - 1, k] for k in range(4)]
        t = mm(jnp.concatenate(blocks, axis=1), order).astype(BF)
        for s in range(3):
            for zi in range(4):
                v = t[s * 16 : s * 16 + 16, zi * 128 : zi * 128 + 128]
                base = (2 * s + zi // 2) * 960 + (2 * wb + zi % 2) * 48
                sp_ref[base : base + 48, :] = spread_x(v)

    def mid(yp, _):
        outs = []
        for zo in range(4):
            i = zo % 2 * 9 + yp
            low, high = (far_ref, near_ref) if zo < 2 else (near_ref, far_ref)
            part = jnp.where(odd, high[i], low[i])
            outs.append(mm(w1_ref[...], window(sp_ref, zo, 2 * yp, 48, 960)) + part)
        keep = [(yp > 0) | (n > 0), (yp < 8) | (n < 3)]
        for zo in range(4):
            v = jnp.maximum(outs[zo], 0.0)
            for k in range(2):
                inside = keep[k] & (w > 0) if zo == 0 else keep[k] & (w < 31) if zo == 3 else keep[k]
                m = jnp.where(inside, v[:, k * 128 : k * 128 + 128], 0.0).astype(BF)
                sm_ref[pl.ds(pl.multiple_of(zo * 3456 + (2 * yp + k) * 192, 64), 192), :] = spread_x(m)
        return 0

    lax.fori_loop(0, 9, mid, 0)
    bias = b_ref[...]
    proj = proj_ref[...]

    def last(i, _):
        outs = [mm(w2_ref[...], window(sm_ref, z, 4 * i + 2 * h, 192, 3456)) for z in range(2) for h in range(2)]
        for j in range(4):
            z, b = j // 2, 2 * i + j % 2
            o = jnp.maximum(outs[j] + bias, 0.0).astype(BF)
            ct = mm(proj, o).astype(BF)
            for k in range(2):
                lanes = slice(k * 128, k * 128 + 128)
                co_ref[pl.ds(pl.multiple_of((2 * b + k) * 64, 64), 64), z * 128 : z * 128 + 128] = o[:, lanes]
                at = (z * 2 + k) * 128
                ct_ref[pl.ds(pl.multiple_of(b * 16, 16), 16), at : at + 128] = ct[:, lanes]
        return 0

    lax.fori_loop(0, 4, last, 0)
    back = onehot((c % 128 // 32 == r // 128) & (c // 128 == r % 128 // 32) & (r % 32 == c % 32))
    ct = mm(ct_ref[...], back).astype(BF)
    for b in range(8):
        for k in range(4):
            block = ct[b * 16 : b * 16 + 16, k * 128 : k * 128 + 128]
            for to in range(4):
                ctx_ref[to, b, k] = jnp.where(n == to, block, jnp.zeros((), BF))
    r, k = iota((256, 256), 0), iota((256, 256), 1)
    perm = onehot((r % 16) * 16 + r // 16 == k)
    for g in range(4):
        rows = jnp.concatenate([co_ref[y * 64 + g * 16 : y * 64 + g * 16 + 16, :] for y in range(16)], axis=0)
        o = mm(perm, rows).astype(BF)
        for z in range(2):
            out_ref[g * 16 : g * 16 + 16, z] = o[:, z * 128 : z * 128 + 128].reshape(16, 16, 128)


def coarse(at, got, near, far, k1, k2, b2, proj):
    def whole(shape):
        return pl.BlockSpec(shape, lambda i, at: (0,) * len(shape))

    return pl.pallas_call(
        coarse_body,
        grid_spec=pltpu.PrefetchScalarGridSpec(
            num_scalar_prefetch=1,
            grid=(1,),
            in_specs=[
                pl.BlockSpec((8, 4, 48, 128), lambda i, at: (at[2], 0, 0, 0)),
                pl.BlockSpec((1, 4, 48, 128), lambda i, at: (jnp.maximum(8 * at[2] - 1, 0), 0, 0, 0)),
                pl.BlockSpec((1, 4, 48, 128), lambda i, at: (jnp.minimum(8 * at[2] + 8, 31), 0, 0, 0)),
                whole((18, 64, 256)),
                whole((18, 64, 256)),
                whole((27, 64, 80)),
                whole((27, 64, 64)),
                whole((64, 1)),
                whole((16, 64)),
            ],
            out_specs=[whole((64, 2, 16, 128)), whole((4, 8, 4, 16, 128))],
            scratch_shapes=[
                pltpu.VMEM((6 * 20 * 48, 128), BF),
                pltpu.VMEM((4 * 18 * 192, 128), BF),
                pltpu.VMEM((64, 432), BF),
                pltpu.VMEM((64, 1728), BF),
                pltpu.VMEM((1024, 256), BF),
                pltpu.VMEM((128, 512), BF),
            ],
        ),
        out_shape=[
            jax.ShapeDtypeStruct((64, 2, 16, 128), BF),
            jax.ShapeDtypeStruct((4, 8, 4, 16, 128), BF),
        ],
        interpret=INTERPRET,
        name="coarse",
    )(at, got, got, got, near, far, k1, k2, b2, proj)


def shift(array, axis, by):
    count = lax.axis_size(axis)
    return lax.ppermute(array, axis, [(i, (i + by) % count) for i in range(count)])


def across_y(rows, from_left, from_right):
    down = jnp.concatenate([rows[:, 112:128, :].reshape(1024, 128), from_left[112:128], from_right[112:128]], axis=0)
    up = jnp.concatenate([rows[:, 0:16, :].reshape(1024, 128), from_left[0:16], from_right[0:16]], axis=0)
    return shift(down, "wide", 1), shift(up, "wide", -1)


def taps(w):
    return jnp.transpose(w, (2, 3, 4, 0, 1)).reshape(27, w.shape[0], w.shape[1])


def local(
    fine_in,
    coarse_in,
    w_fine1,
    b_fine1,
    w_fine2,
    b_fine2,
    w_coarse1,
    b_coarse1,
    w_coarse2,
    b_coarse2,
    w_proj,
):
    w = lax.axis_index("wide")
    n = lax.axis_index("narrow")
    reaches = jnp.where(w % 2 == 1, w < 31, w > 0).astype(jnp.int32)
    at = jnp.stack([w // 8, w % 8, n, w, w % 2, reaches])
    rows, cols = prep(fine_in)
    ct = cprep(coarse_in)
    east = jnp.concatenate([cols, ct[:, 14:16].reshape(256, 128)], axis=0)
    west = jnp.concatenate([cols, ct[:, 0:2].reshape(256, 128)], axis=0)
    from_left = shift(east, "narrow", 1)
    from_right = shift(west, "narrow", -1)
    top, bottom = across_y(rows, from_left, from_right)
    slab = jnp.concatenate(
        [
            jnp.where(n > 0, from_left[128:], jnp.zeros((), BF)).reshape(2, 2, 64, 128),
            ct,
            jnp.where(n < 3, from_right[128:], jnp.zeros((), BF)).reshape(2, 2, 64, 128),
        ],
        axis=1,
    )
    mate = lax.ppermute(slab, "wide", [(i, i ^ 1) for i in range(32)])
    hops = [(i, i + 2 - 4 * (i % 2)) for i in range(32)]
    far = lax.ppermute(mate, "wide", [(i, j % 32) for i, j in hops])
    hidden, parcels, hcols = fine1(
        at, rows, top, bottom, from_left, from_right, taps(w_fine1), b_fine1[None]
    )
    got = lax.all_to_all(parcels.reshape(128, 48, 128), ("wide", "narrow"), 0, 0, tiled=True)
    near_part = conv1a(at, slab, mate, taps(w_coarse1), b_coarse1[:, None], "near")
    hleft = shift(hcols, "narrow", 1)
    hright = shift(hcols, "narrow", -1)
    htop, hbottom = across_y(hidden, hleft, hright)
    far_part = conv1a(at, far, slab, taps(w_coarse1), b_coarse1[:, None], "distant")
    coarse_out, context = coarse(
        at,
        got.reshape(32, 4, 48, 128),
        near_part,
        far_part,
        taps(w_coarse1),
        taps(w_coarse2),
        b_coarse2[:, None],
        w_proj,
    )
    arrived = lax.all_to_all(context.reshape(128, 16, 128), ("wide", "narrow"), 0, 0, tiled=True)
    fine_out = fine2(
        at,
        hidden,
        htop,
        hbottom,
        hleft,
        hright,
        taps(w_fine2),
        b_fine2[None],
        arrived.reshape(32, 4, 16, 128),
    )
    return fine_out, coarse_out


def solution(mesh):
    return jax.shard_map(
        local,
        mesh=mesh,
        in_specs=(P(None, None, "wide", "narrow"), P(None, "wide", "narrow", None)) + (P(),) * 9,
        out_specs=(P(None, None, "wide", "narrow"), P(None, "wide", "narrow", None)),
        check_vma=False,
    )
```

profile of v0, /device:TPU:1, one launch (start us, length us, event | category | flops | bytes accessed | tf_op | source)
XLA Modules:
  0.0 171.3 jit_solution(2360696374813641251)
XLA Ops:
  0.6 6.2 %prep.1 = (bf16[64,128,128]{2,1,0:T(8,128)(2,1)}, bf16[128,128]{1,0:T(8,128)(2,1)}) custom-call(bf16[16,64,8,128]{3,2,1,0:T(8,128)(2,1)} %x_ref.2), custom_call_target="tpu_custom_call" | custom-call | tf_op jit(solution)/shard_map/prep/pallas_call | solution.py:66
  6.8 2.1 %cprep.1 = bf16[2,16,64,128]{3,2,1,0:T(8,128)(2,1)} custom-call(bf16[64,2,16,128]{3,2,1,0:T(8,128)(2,1)} %x_ref.3), custom_call_target="tpu_custom_call" | custom-call | tf_op jit(solution)/shard_map/cprep/pallas_call | solution.py:95
  9.0 0.9 fusion.2
  9.9 0.8 pad_maximum_fusion.6
  10.6 1.4 collective-permute-start.1
  12.1 3.0 %collective-permute-start = (bf16[384,128]{1,0:T(8,128)(2,1)S(1)}, bf16[384,128]{1,0:T(8,128)(2,1)S(1)}, u32[]{:S(2)}, u32[]{:S(2)}) collective-permute-start(bf16[384,128]{1,0:T(8,128)(2,1)S(1)} %get-tuple-element.30), channel_id=1, source_target_pairs={{0,1},{1,2},{2,3},{3,0},{4,5},{5,6},{6,7},{7,4},{8,9},{9,10},{10,1... | collective-permute-start | bytes 294920 | tf_op jit(solution)/shard_map/ppermute | solution.py:470
  15.1 1.1 fusion.1
  16.2 1.1 collective-permute-done.1.cr_ref
  17.7 0.8 collective-permute-start.2
  18.5 5.8 %collective-permute-start.3 = (bf16[1056,128]{1,0:T(8,128)(2,1)S(1)}, bf16[1056,128]{1,0:T(8,128)(2,1)S(1)}, u32[]{:S(2)}, u32[]{:S(2)}) collective-permute-start(bf16[1056,128]{1,0:T(8,128)(2,1)S(1)} %pad_maximum_fusion.2), channel_id=1, source_target_pairs={{0,124},{4,0},{8,4},{12,8},{16,12},{20,16},{24,20},{28,24},{32,28}... | collective-permute-start | bytes 811016 | tf_op jit(solution)/shard_map/ppermute | solution.py:470
  24.9 3.8 %collective-permute-done.2.top_ref = bf16[1056,128]{1,0:T(8,128)(2,1)S(1)} collective-permute-done((bf16[1056,128]{1,0:T(8,128)(2,1)S(1)}, bf16[1056,128]{1,0:T(8,128)(2,1)S(1)}, u32[]{:S(2)}, u32[]{:S(2)}) %collective-permute-start.2) | collective-permute-done | bytes 270368 | tf_op jit(solution)/shard_map/ppermute | solution.py:470
  28.7 1.6 collective-permute-done.3.bot_ref
  30.3 0.7 copy-done.11
  31.0 11.0 %fine1.1 = (bf16[64,128,128]{2,1,0:T(8,128)(2,1)}, bf16[32,4,48,128]{3,2,1,0:T(8,128)(2,1)}, bf16[128,128]{1,0:T(8,128)(2,1)}) custom-call(s32[6]{0:T(128)} %stack.31.at_ref, bf16[64,128,128]{2,1,0:T(8,128)(2,1)} %get-tuple-element.9.x_ref, bf16[1056,128]{1,0:T(8,128)(2,1)} %copy-done.10, bf16[1056,128]{1,0:T(8,128)(2,1)} %copy-done.11, ...), custom_call_target="tpu_custom_call" | custom-call | tf_op jit(solution)/shard_map/fine1/pallas_call | solution.py:234
  42.0 13.8 %all-to-all-start = ((bf16[128,48,128]{2,1,0:T(8,128)(2,1)}), bf16[128,48,128]{2,1,0:T(8,128)(2,1)S(1)}, u32[]{:S(2)}, u32[]{:S(2)}) async-start(bf16[128,48,128]{2,1,0:T(8,128)(2,1)} %bitcast.41), calls=%async_computation | async-start | bytes 3145728 | tf_op jit(solution)/shard_map/all_to_all | solution.py:521
  56.0 1.4 collective-permute-start.8
  57.4 0.7 copy.13.b_ref
  59.5 2.6 %collective-permute-start.4 = (bf16[128,128]{1,0:T(8,128)(2,1)S(1)}, bf16[128,128]{1,0:T(8,128)(2,1)S(1)}, u32[]{:S(2)}, u32[]{:S(2)}) collective-permute-start(bf16[128,128]{1,0:T(8,128)(2,1)S(1)} %copy-done.16), channel_id=1, source_target_pairs={{0,1},{1,2},{2,3},{3,0},{4,5},{5,6},{6,7},{7,4},{8,9},{9,10},{10,1... | collective-permute-start | bytes 98312 | tf_op jit(solution)/shard_map/ppermute | solution.py:470
  62.1 26.0 %collective-permute-done.8.second_ref = bf16[2,20,64,128]{3,2,1,0:T(8,128)(2,1)S(1)} collective-permute-done((bf16[2,20,64,128]{3,2,1,0:T(8,128)(2,1)S(1)}, bf16[2,20,64,128]{3,2,1,0:T(8,128)(2,1)S(1)}, u32[]{:S(2)}, u32[]{:S(2)}) %collective-permute-start.8) | collective-permute-done | bytes 655392 | tf_op jit(solution)/shard_map/ppermute | solution.py:515
  88.1 1.4 collective-permute-start.9
  89.5 1.1 fusion
  90.6 7.9 %shard_map.122.near_ref = f32[18,64,256]{2,1,0:T(8,128)} custom-call(s32[6]{0:T(128)} %stack.31.at_ref, bf16[2,20,64,128]{3,2,1,0:T(8,128)(2,1)} %copy-done.1, bf16[2,20,64,128]{3,2,1,0:T(8,128)(2,1)} %copy-done.4, bf16[27,64,80]{2,1,0:T(8,128)(2,1)} %bitcast.37, f32[64,1]{1,0:T(8,128)} %copy.13.b_ref), custom_call_target="tpu_custom_call" | custom-call | tf_op jit(solution)/shard_map/pallas_call | solution.py:347
  98.5 9.7 %collective-permute-done.9.first_ref = bf16[2,20,64,128]{3,2,1,0:T(8,128)(2,1)} collective-permute-done((bf16[2,20,64,128]{3,2,1,0:T(8,128)(2,1)S(1)}, bf16[2,20,64,128]{3,2,1,0:T(8,128)(2,1)}, u32[]{:S(2)}, u32[]{:S(2)}) %collective-permute-start.9) | collective-permute-done | bytes 655392 | tf_op jit(solution)/shard_map/ppermute | solution.py:517
  108.2 7.9 %shard_map.123.far_ref = f32[18,64,256]{2,1,0:T(8,128)} custom-call(s32[6]{0:T(128)} %stack.31.at_ref, bf16[2,20,64,128]{3,2,1,0:T(8,128)(2,1)} %collective-permute-done.9.first_ref, bf16[2,20,64,128]{3,2,1,0:T(8,128)(2,1)} %copy-done.1, bf16[27,64,80]{2,1,0:T(8,128)(2,1)} %bitcast.38, f32[64,1]{1,0:T(8,128)} %copy.13.b_ref), custom_call_target="tpu_custom_call" | custom-call | tf_op jit(solution)/shard_map/pallas_call | solution.py:347
  116.2 1.1 copy-done
  117.3 13.8 %coarse.1 = (bf16[64,2,16,128]{3,2,1,0:T(8,128)(2,1)}, bf16[4,8,4,16,128]{4,3,2,1,0:T(8,128)(2,1)}) custom-call(s32[6]{0:T(128)} %stack.31.at_ref, bf16[32,4,48,128]{3,2,1,0:T(8,128)(2,1)} %bitcast.34, bf16[32,4,48,128]{3,2,1,0:T(8,128)(2,1)} %bitcast.35, bf16[32,4,48,128]{3,2,1,0:T(8,128)(2,1)} %bitcast.36, f32[18,64,256]{2,1,0:T(8,128)} %shard_map.122.near_ref, ...), custom_call_target="tpu_custom_call" | custom-call | tf_op jit(solution)/shard_map/coarse/pallas_call | solution.py:433
  131.1 8.7 %all-to-all-start.1 = ((bf16[128,16,128]{2,1,0:T(8,128)(2,1)}), bf16[128,16,128]{2,1,0:T(8,128)(2,1)S(1)}, u32[]{:S(2)}, u32[]{:S(2)}) async-start(bf16[128,16,128]{2,1,0:T(8,128)(2,1)} %bitcast.46), calls=%async_computation.1 | async-start | bytes 1048576 | tf_op jit(solution)/shard_map/all_to_all | solution.py:537
  139.8 1.4 collective-permute-start.6
  141.3 5.1 %collective-permute-start.7 = (bf16[1056,128]{1,0:T(8,128)(2,1)S(1)}, bf16[1056,128]{1,0:T(8,128)(2,1)S(1)}, u32[]{:S(2)}, u32[]{:S(2)}) collective-permute-start(bf16[1056,128]{1,0:T(8,128)(2,1)S(1)} %pad_maximum_fusion.4), channel_id=1, source_target_pairs={{0,124},{4,0},{8,4},{12,8},{16,12},{20,16},{24,20},{28,24},{32,28}... | collective-permute-start | bytes 811016 | tf_op jit(solution)/shard_map/ppermute | solution.py:470
  146.4 11.6 %collective-permute-done.6.top_ref = bf16[1056,128]{1,0:T(8,128)(2,1)S(1)} collective-permute-done((bf16[1056,128]{1,0:T(8,128)(2,1)S(1)}, bf16[1056,128]{1,0:T(8,128)(2,1)S(1)}, u32[]{:S(2)}, u32[]{:S(2)}) %collective-permute-start.6) | collective-permute-done | bytes 270368 | tf_op jit(solution)/shard_map/ppermute | solution.py:470
  158.0 1.6 collective-permute-done.7.bot_ref
  160.5 10.8 %fine2.1 = bf16[16,64,8,128]{3,2,1,0:T(8,128)(2,1)} custom-call(s32[6]{0:T(128)} %stack.31.at_ref, bf16[64,128,128]{2,1,0:T(8,128)(2,1)} %get-tuple-element.11.x_ref, bf16[1056,128]{1,0:T(8,128)(2,1)} %copy-done.8, bf16[1056,128]{1,0:T(8,128)(2,1)} %copy-done.9, bf16[128,128]{1,0:T(8,128)(2,1)} %copy-done.13, bf16[128,128]{1,0:T(8,128)(2,1)} %copy-done.12, ...), custom_call_target="tpu_custom_call" | custom-call | tf_op jit(solution)/shard_map/fine2/pallas_call | solution.py:276
  (51 shorter events, 3.6 us)
Async XLA Ops:
  10.6 6.7 %collective-permute-start.1 = (bf16[384,128]{1,0:T(8,128)(2,1)S(1)}, bf16[384,128]{1,0:T(8,128)(2,1)S(1)}, u32[]{:S(2)}, u32[]{:S(2)}) collective-permute-start(bf16[384,128]{1,0:T(8,128)(2,1)S(1)} %get-tuple-element.31), channel_id=1, source_target_pairs={{0,3},{1,0},{2,1},{3,2},{4,7},{5,4},{6,5},{7,6},{8,11},{9,8},{10,9... | collective-permute-start | bytes 294920 | tf_op jit(solution)/shard_map/ppermute | solution.py:470
  12.1 5.6 %collective-permute-start = (bf16[384,128]{1,0:T(8,128)(2,1)S(1)}, bf16[384,128]{1,0:T(8,128)(2,1)S(1)}, u32[]{:S(2)}, u32[]{:S(2)}) collective-permute-start(bf16[384,128]{1,0:T(8,128)(2,1)S(1)} %get-tuple-element.30), channel_id=1, source_target_pairs={{0,1},{1,2},{2,3},{3,0},{4,5},{5,6},{6,7},{7,4},{8,9},{9,10},{10,1... | collective-permute-start | bytes 294920 | tf_op jit(solution)/shard_map/ppermute | solution.py:470
  17.3 13.0 %copy-start.7 = (bf16[384,128]{1,0:T(8,128)(2,1)}, bf16[384,128]{1,0:T(8,128)(2,1)S(1)}, u32[]{:S(2)}) copy-start(bf16[384,128]{1,0:T(8,128)(2,1)S(1)} %collective-permute-done.1.cr_ref) | copy-start | bytes 294916
  17.7 12.6 %copy-start.5 = (bf16[384,128]{1,0:T(8,128)(2,1)}, bf16[384,128]{1,0:T(8,128)(2,1)S(1)}, u32[]{:S(2)}) copy-start(bf16[384,128]{1,0:T(8,128)(2,1)S(1)} %collective-permute-done.cl_ref) | copy-start | bytes 294916
  17.7 11.0 %collective-permute-start.2 = (bf16[1056,128]{1,0:T(8,128)(2,1)S(1)}, bf16[1056,128]{1,0:T(8,128)(2,1)S(1)}, u32[]{:S(2)}, u32[]{:S(2)}) collective-permute-start(bf16[1056,128]{1,0:T(8,128)(2,1)S(1)} %pad_maximum_fusion.1), channel_id=1, source_target_pairs={{0,4},{4,8},{8,12},{12,16},{16,20},{20,24},{24,28},{28,32},{32,36}... | collective-permute-start | bytes 811016 | tf_op jit(solution)/shard_map/ppermute | solution.py:470
  18.5 11.8 %collective-permute-start.3 = (bf16[1056,128]{1,0:T(8,128)(2,1)S(1)}, bf16[1056,128]{1,0:T(8,128)(2,1)S(1)}, u32[]{:S(2)}, u32[]{:S(2)}) collective-permute-start(bf16[1056,128]{1,0:T(8,128)(2,1)S(1)} %pad_maximum_fusion.2), channel_id=1, source_target_pairs={{0,124},{4,0},{8,4},{12,8},{16,12},{20,16},{24,20},{28,24},{32,28}... | collective-permute-start | bytes 811016 | tf_op jit(solution)/shard_map/ppermute | solution.py:470
  28.7 1.6 copy-start.10
  30.3 0.7 copy-start.11
  42.0 13.8 %copy-start.6 = (bf16[384,128]{1,0:T(8,128)(2,1)S(1)}, bf16[384,128]{1,0:T(8,128)(2,1)}, u32[]{:S(2)}) copy-start(bf16[384,128]{1,0:T(8,128)(2,1)} %copy-done.5) | copy-start | bytes 294916
  42.0 13.8 %copy-start.2 = (bf16[2,16,64,128]{3,2,1,0:T(8,128)(2,1)S(1)}, bf16[2,16,64,128]{3,2,1,0:T(8,128)(2,1)}, u32[]{:S(2)}) copy-start(bf16[2,16,64,128]{3,2,1,0:T(8,128)(2,1)} %cprep.1) | copy-start | bytes 1572868
  42.0 15.4 %copy-start.14 = (f32[64]{0:T(128)S(1)}, f32[64]{0:T(128)}, u32[]{:S(2)}) copy-start(f32[64]{0:T(128)} %param.18) | copy-start | bytes 772
  42.0 16.1 %copy-start.15 = (f32[64]{0:T(128)S(1)}, f32[64]{0:T(128)}, u32[]{:S(2)}) copy-start(f32[64]{0:T(128)} %param.20) | copy-start | bytes 772
  42.0 16.8 %copy-start.16 = (bf16[128,128]{1,0:T(8,128)(2,1)S(1)}, bf16[128,128]{1,0:T(8,128)(2,1)}, u32[]{:S(2)}) copy-start(bf16[128,128]{1,0:T(8,128)(2,1)} %get-tuple-element.12) | copy-start | bytes 98308
  42.0 74.1 %all-to-all-start = ((bf16[128,48,128]{2,1,0:T(8,128)(2,1)}), bf16[128,48,128]{2,1,0:T(8,128)(2,1)S(1)}, u32[]{:S(2)}, u32[]{:S(2)}) async-start(bf16[128,48,128]{2,1,0:T(8,128)(2,1)} %bitcast.41), calls=%async_computation | async-start | bytes 3145728 | tf_op jit(solution)/shard_map/all_to_all | solution.py:521
  55.9 34.7 %copy-start.1 = (bf16[2,20,64,128]{3,2,1,0:T(8,128)(2,1)}, bf16[2,20,64,128]{3,2,1,0:T(8,128)(2,1)S(1)}, u32[]{:S(2)}) copy-start(bf16[2,20,64,128]{3,2,1,0:T(8,128)(2,1)S(1)} %pad_maximum_fusion.first_ref.second_ref) | copy-start | bytes 1966084
  56.0 32.1 %collective-permute-start.8 = (bf16[2,20,64,128]{3,2,1,0:T(8,128)(2,1)S(1)}, bf16[2,20,64,128]{3,2,1,0:T(8,128)(2,1)S(1)}, u32[]{:S(2)}, u32[]{:S(2)}) collective-permute-start(bf16[2,20,64,128]{3,2,1,0:T(8,128)(2,1)S(1)} %pad_maximum_fusion.first_ref.second_ref), channel_id=1, source_target_pairs={{0,4},{4,0},{8,12},{12,8},{16,20},{20,16},{24,28},{28,24},{32,36},... | collective-permute-start | bytes 1966088 | tf_op jit(solution)/shard_map/ppermute | solution.py:515
  58.8 31.8 %collective-permute-start.5 = (bf16[128,128]{1,0:T(8,128)(2,1)S(1)}, bf16[128,128]{1,0:T(8,128)(2,1)S(1)}, u32[]{:S(2)}, u32[]{:S(2)}) collective-permute-start(bf16[128,128]{1,0:T(8,128)(2,1)S(1)} %copy-done.16), channel_id=1, source_target_pairs={{0,3},{1,0},{2,1},{3,2},{4,7},{5,4},{6,5},{7,6},{8,11},{9,8},{10,9... | collective-permute-start | bytes 98312 | tf_op jit(solution)/shard_map/ppermute | solution.py:470
  59.5 31.1 %collective-permute-start.4 = (bf16[128,128]{1,0:T(8,128)(2,1)S(1)}, bf16[128,128]{1,0:T(8,128)(2,1)S(1)}, u32[]{:S(2)}, u32[]{:S(2)}) collective-permute-start(bf16[128,128]{1,0:T(8,128)(2,1)S(1)} %copy-done.16), channel_id=1, source_target_pairs={{0,1},{1,2},{2,3},{3,0},{4,5},{5,6},{6,7},{7,4},{8,9},{9,10},{10,1... | collective-permute-start | bytes 98312 | tf_op jit(solution)/shard_map/ppermute | solution.py:470
  88.1 2.5 %copy-start.4 = (bf16[2,20,64,128]{3,2,1,0:T(8,128)(2,1)}, bf16[2,20,64,128]{3,2,1,0:T(8,128)(2,1)S(1)}, u32[]{:S(2)}) copy-start(bf16[2,20,64,128]{3,2,1,0:T(8,128)(2,1)S(1)} %collective-permute-done.8.second_ref) | copy-start | bytes 1966084
  88.1 20.1 %collective-permute-start.9 = (bf16[2,20,64,128]{3,2,1,0:T(8,128)(2,1)S(1)}, bf16[2,20,64,128]{3,2,1,0:T(8,128)(2,1)}, u32[]{:S(2)}, u32[]{:S(2)}) collective-permute-start(bf16[2,20,64,128]{3,2,1,0:T(8,128)(2,1)S(1)} %collective-permute-done.8.second_ref), channel_id=1, source_target_pairs={{0,8},{4,124},{8,16},{12,4},{16,24},{20,12},{24,32},{28,20},{32,40... | collective-permute-start | bytes 1966088 | tf_op jit(solution)/shard_map/ppermute | solution.py:517
  90.6 25.6 %copy-start.12 = (bf16[128,128]{1,0:T(8,128)(2,1)}, bf16[128,128]{1,0:T(8,128)(2,1)S(1)}, u32[]{:S(2)}) copy-start(bf16[128,128]{1,0:T(8,128)(2,1)S(1)} %collective-permute-done.5.cr_ref) | copy-start | bytes 98308
  90.6 25.6 %copy-start.13 = (bf16[128,128]{1,0:T(8,128)(2,1)}, bf16[128,128]{1,0:T(8,128)(2,1)S(1)}, u32[]{:S(2)}) copy-start(bf16[128,128]{1,0:T(8,128)(2,1)S(1)} %collective-permute-done.4.cl_ref) | copy-start | bytes 98308
  116.1 1.1 copy-start
  131.1 28.5 %all-to-all-start.1 = ((bf16[128,16,128]{2,1,0:T(8,128)(2,1)}), bf16[128,16,128]{2,1,0:T(8,128)(2,1)S(1)}, u32[]{:S(2)}, u32[]{:S(2)}) async-start(bf16[128,16,128]{2,1,0:T(8,128)(2,1)} %bitcast.46), calls=%async_computation.1 | async-start | bytes 1048576 | tf_op jit(solution)/shard_map/all_to_all | solution.py:537
  139.8 18.1 %collective-permute-start.6 = (bf16[1056,128]{1,0:T(8,128)(2,1)S(1)}, bf16[1056,128]{1,0:T(8,128)(2,1)S(1)}, u32[]{:S(2)}, u32[]{:S(2)}) collective-permute-start(bf16[1056,128]{1,0:T(8,128)(2,1)S(1)} %pad_maximum_fusion.3), channel_id=1, source_target_pairs={{0,4},{4,8},{8,12},{12,16},{16,20},{20,24},{24,28},{28,32},{32,36}... | collective-permute-start | bytes 811016 | tf_op jit(solution)/shard_map/ppermute | solution.py:470
  141.3 18.3 %collective-permute-start.7 = (bf16[1056,128]{1,0:T(8,128)(2,1)S(1)}, bf16[1056,128]{1,0:T(8,128)(2,1)S(1)}, u32[]{:S(2)}, u32[]{:S(2)}) collective-permute-start(bf16[1056,128]{1,0:T(8,128)(2,1)S(1)} %pad_maximum_fusion.4), channel_id=1, source_target_pairs={{0,124},{4,0},{8,4},{12,8},{16,12},{20,16},{24,20},{28,24},{32,28}... | collective-permute-start | bytes 811016 | tf_op jit(solution)/shard_map/ppermute | solution.py:470
  158.0 1.6 copy-start.8
  159.6 0.7 copy-start.9
  159.6 0.9 copy-start.3
where the time goes:
time: 172 us; the launch traced here: 171 us
  Pallas kernels  59.7 us (35%)
  waiting for transfers between devices  55.9 us (32%)
  starting transfers between devices  46.1 us (27%)
  local copies, waits for them, and re-layouts  7.9 us (5%)
    ppermute x1, waiting for transfers between devices, local(): mate = lax.ppermute(slab, 'wide', [(i, i ^ 1) for i in range(32)])  26 us
    ppermute x8, starting transfers between devices, shift(): lax.ppermute(array, axis, [(i, (i + by) % count) for i in range(count)])  20.7 us
    ppermute x8, waiting for transfers between devices, shift(): lax.ppermute(array, axis, [(i, (i + by) % count) for i in range(count)])  20.1 us
    pallas_call x2, Pallas kernels, conv1a(): pl.pallas_call(functools.partial(conv1a_body, name == 'distant'), in_spec...  15.8 us
    all_to_all x1, starting transfers between devices, local(): lax.all_to_all(parcels.reshape(128, 48, 128), ('wide', 'narrow'), 0, 0, t...  13.8 us
    pallas_call x1, Pallas kernels, coarse(): pl.pallas_call(coarse_body, grid_spec=pltpu.PrefetchScalarGridSpec(num_sc...  13.8 us
    pallas_call x1, Pallas kernels, fine1(): pl.pallas_call(fine1_body, in_specs=[pl.BlockSpec(memory_space=pltpu.SMEM...  11 us
    pallas_call x1, Pallas kernels, fine2(): pl.pallas_call(fine2_body, grid_spec=pltpu.PrefetchScalarGridSpec(num_sca...  10.8 us
  transfers between devices with their start and end apart: 12, of which 8 were waited for; matrix products, arithmetic and copies ran while one was open for 3% of the time, Pallas kernels for 9%

commit v1 on v0

v1 whole, which is shorter than its diff:
```python
import functools

import jax
import jax.numpy as jnp
from jax import lax
from jax.experimental import pallas as pl
from jax.experimental.pallas import tpu as pltpu
from jax.sharding import PartitionSpec as P


BF = jnp.bfloat16
F32 = jnp.float32
TERM = jnp.bfloat16
INTERPRET = False


def iota(shape, axis):
    return lax.broadcasted_iota(jnp.int32, shape, axis)


def onehot(mask):
    return jnp.where(mask, 1.0, 0.0).astype(BF)


def mm(a, b):
    return jnp.dot(a, b, preferred_element_type=F32)


def vm(n):
    return [pl.BlockSpec(memory_space=pltpu.VMEM)] * n


def outer_columns(rows, first_z):
    shape = (rows.shape[1], 128)
    r, lane = iota(shape, 0), iota(shape, 1)
    z, x = first_z + r // 128, r % 128
    return mm(rows, onehot(((x == 0) & (lane == z)) | ((x == 127) & (lane == z + 64))))


def prep_body(x_ref, t_ref, down_ref, up_ref, cols_ref, acc_ref):
    step = pl.program_id(0)
    zb = t_ref.shape[0]
    r, k = iota((128, 128), 0), iota((128, 128), 1)
    perm = onehot((r % 16) * 8 + r // 16 == k)
    rows = []
    for i in range(0, zb, 2):
        pair = jnp.concatenate([x_ref[:, step * zb + i + j].reshape(128, 128) for j in range(2)], axis=1)
        out = mm(perm, pair).astype(BF)
        for j in range(2):
            v = out[:, j * 128 : j * 128 + 128]
            t_ref[i + j] = v
            down_ref[(i + j) * 16 : (i + j) * 16 + 16, :] = v[112:128]
            up_ref[(i + j) * 16 : (i + j) * 16 + 16, :] = v[0:16]
        rows.append(out)
    part = outer_columns(jnp.concatenate(rows, axis=1), step * zb)

    @pl.when(step == 0)
    def _():
        acc_ref[...] = part

    @pl.when(step > 0)
    def _():
        acc_ref[...] += part

    cols_ref[...] = acc_ref[...].astype(BF)


def prep(x):
    zb = 8
    return pl.pallas_call(
        prep_body,
        grid=(64 // zb,),
        in_specs=[pl.BlockSpec((16, 64, 8, 128), lambda i: (0, 0, 0, 0))],
        out_specs=[
            pl.BlockSpec((zb, 128, 128), lambda i: (i, 0, 0)),
            pl.BlockSpec((zb * 16, 128), lambda i: (i, 0)),
            pl.BlockSpec((zb * 16, 128), lambda i: (i, 0)),
            pl.BlockSpec((128, 128), lambda i: (0, 0)),
        ],
        out_shape=[
            jax.ShapeDtypeStruct((64, 128, 128), BF),
            jax.ShapeDtypeStruct((1056, 128), BF),
            jax.ShapeDtypeStruct((1056, 128), BF),
            jax.ShapeDtypeStruct((128, 128), BF),
        ],
        scratch_shapes=[pltpu.VMEM((128, 128), F32)],
        interpret=INTERPRET,
        name="prep",
    )(x)


def cprep_body(x_ref, cols_ref, o_ref, east_ref, west_ref):
    east_ref[0:128, :] = cols_ref[...]
    west_ref[0:128, :] = cols_ref[...]
    r, k = iota((256, 256), 0), iota((256, 256), 1)
    perm = onehot((r % 16) * 16 + r // 16 == k)
    for g in range(4):
        pair = jnp.concatenate(
            [x_ref[g * 16 : g * 16 + 16, z].reshape(256, 128) for z in range(2)], axis=1
        )
        out = mm(perm, pair).astype(BF)
        for z in range(2):
            for y in range(16):
                v = out[y * 16 : y * 16 + 16, z * 128 : z * 128 + 128]
                o_ref[z, y, g * 16 : g * 16 + 16, :] = v
                row = 128 + z * 128 + (y % 2) * 64 + g * 16
                if y >= 14:
                    east_ref[row : row + 16, :] = v
                if y < 2:
                    west_ref[row : row + 16, :] = v


def cprep(x, cols):
    return pl.pallas_call(
        cprep_body,
        in_specs=vm(2),
        out_specs=vm(3),
        out_shape=[
            jax.ShapeDtypeStruct((2, 16, 64, 128), BF),
            jax.ShapeDtypeStruct((384, 128), BF),
            jax.ShapeDtypeStruct((384, 128), BF),
        ],
        interpret=INTERPRET,
        name="cprep",
    )(x, cols)


def weights_body(f1_ref, f2_ref, c1_ref, c2_ref, wf1_ref, wf2_ref, wa_ref, wb_ref, wc_ref, w0_ref):
    for k_ref, w_ref in ((f1_ref, wf1_ref), (f2_ref, wf2_ref)):
        w0_ref[...] = jnp.zeros((16, 1536), F32)
        for t in range(27):
            dz, dy, dx = t // 9, t // 3 % 3, t % 3
            at = dz * 512 + dx * 160 + dy * 16
            w0_ref[:, at : at + 16] = k_ref[t].astype(F32)
        w0 = w0_ref[...]
        for y in range(8):
            w_ref[y * 16 : y * 16 + 16, :] = (pltpu.roll(w0, y * 16, 1) if y else w0).astype(BF)
    r, k = iota((128, 128), 0), iota((128, 128), 1)
    wf2_ref[...] = mm(onehot((r % 8) * 16 + r // 8 == k), wf2_ref[...]).astype(BF)
    for t in range(27):
        both = c1_ref[t]
        wa_ref[:, t * 64 : t * 64 + 64] = both[:, 0:64]
        wb_ref[:, t * 16 : t * 16 + 16] = both[:, 64:80]
        wc_ref[:, t * 64 : t * 64 + 64] = c2_ref[t]


def weights(f1, f2, c1, c2):
    return pl.pallas_call(
        weights_body,
        in_specs=vm(4),
        out_specs=vm(5),
        out_shape=[
            jax.ShapeDtypeStruct((128, 1536), BF),
            jax.ShapeDtypeStruct((128, 1536), BF),
            jax.ShapeDtypeStruct((64, 1728), BF),
            jax.ShapeDtypeStruct((64, 432), BF),
            jax.ShapeDtypeStruct((64, 1728), BF),
        ],
        scratch_shapes=[pltpu.VMEM((16, 1536), F32)],
        interpret=INTERPRET,
        name="weights",
    )(f1, f2, c1, c2)


def kept(ok, v):
    return jnp.where(ok, v, jnp.zeros((), BF))


def stage(z, at_ref, x_ref, top_ref, bot_ref, tl_ref, tr_ref, s_ref):
    rows = pl.ds(pl.multiple_of(z * 16, 16), 16)
    top = kept(at_ref[3] > 0, top_ref[rows, :])
    bot = kept(at_ref[3] < 31, bot_ref[rows, :])
    v = jnp.concatenate([top, x_ref[z], bot], axis=0)
    lane = iota((160, 128), 1)
    left = jnp.where(lane == 0, pltpu.roll(tl_ref[...], lax.rem(192 - z, 128), 1), pltpu.roll(v, 1, 1))
    right = jnp.where(lane == 127, pltpu.roll(tr_ref[...], 127 - z, 1), pltpu.roll(v, 127, 1))
    base = pl.multiple_of((z + 1) * 512, 512)
    s_ref[pl.ds(base, 160), :] = left
    s_ref[pl.ds(base + 160, 160), :] = v
    s_ref[pl.ds(base + 320, 160), :] = right


def conv_pair(z, w_ref, s_ref):
    base = pl.multiple_of(z * 512, 512)
    rhs = jnp.concatenate([s_ref[pl.ds(base, 1536), :], s_ref[pl.ds(base + 512, 1536), :]], axis=1)
    return mm(w_ref[...], rhs)


def bias_rows(b_ref, count, row_of):
    shape = (count, b_ref.shape[1])
    r, k = iota(shape, 0), iota(shape, 1)
    return jnp.sum(jnp.where(row_of(r) == k, b_ref[...], 0.0), axis=1, keepdims=True)


def fine_setup(at_ref, top_ref, bot_ref, cl_ref, cr_ref, s_ref, tl_ref, tr_ref):
    n, w = at_ref[2], at_ref[3]
    for ref, edge, col, ok in ((tl_ref, 1024, cl_ref, n > 0), (tr_ref, 1040, cr_ref, n < 3)):
        ref[0:16, :] = kept(ok & (w > 0), top_ref[edge : edge + 16, :])
        ref[16:144, :] = kept(ok, col[0:128, :])
        ref[144:160, :] = kept(ok & (w < 31), bot_ref[edge : edge + 16, :])
    s_ref[0:512, :] = jnp.zeros((512, 128), BF)
    s_ref[65 * 512 : 66 * 512, :] = jnp.zeros((512, 128), BF)
    for z in range(1, 65):
        s_ref[z * 512 + 480 : z * 512 + 512, :] = jnp.zeros((32, 128), BF)


def run_conv(stage_fn, finish, w_ref, s_ref):
    for z in range(5):
        stage_fn(z)

    def step(i, _):
        first = conv_pair(4 * i, w_ref, s_ref)
        second = conv_pair(4 * i + 2, w_ref, s_ref)
        for k in range(5, 9):
            stage_fn(4 * i + k)
        finish(2 * i, first)
        finish(2 * i + 1, second)
        return 0

    lax.fori_loop(0, 14, step, 0)
    first = conv_pair(56, w_ref, s_ref)
    second = conv_pair(58, w_ref, s_ref)
    for k in range(61, 64):
        stage_fn(k)
    finish(28, first)
    finish(29, second)
    first = conv_pair(60, w_ref, s_ref)
    second = conv_pair(62, w_ref, s_ref)
    finish(30, first)
    finish(31, second)


def fine1_body(at_ref, x_ref, top_ref, bot_ref, cl_ref, cr_ref, w_ref, b_ref, h_ref, p_ref, cols_ref, down_ref, up_ref, s_ref, tl_ref, tr_ref, acc_ref):
    fine_setup(at_ref, top_ref, bot_ref, cl_ref, cr_ref, s_ref, tl_ref, tr_ref)
    bias = bias_rows(b_ref, 128, lambda r: r % 16)

    def finish(i, out):
        h = jnp.maximum(out + bias, 0.0).astype(BF)
        parts = []
        for k in range(2):
            hz = h[:, k * 128 : (k + 1) * 128]
            h_ref[2 * i + k] = hz
            row = pl.ds(pl.multiple_of((2 * i + k) * 16, 16), 16)
            down_ref[row, :] = hz[112:128]
            up_ref[row, :] = hz[0:16]
            f = hz.astype(F32)
            for half in range(2):
                r = f[half * 64 : half * 64 + 64]
                parts.append((r[0:16] + r[16:32]) + (r[32:48] + r[48:64]))
        hi = [p.astype(BF) for p in parts]
        lo = [(p - q.astype(F32)).astype(BF) for p, q in zip(parts, hi)]
        acc_ref[pl.ds(pl.multiple_of(i * 16, 16), 16), :] = jnp.concatenate(hi + lo, axis=1)

    run_conv(lambda z: stage(z, at_ref, x_ref, top_ref, bot_ref, tl_ref, tr_ref, s_ref), finish, w_ref, s_ref)
    r, lane = iota((1024, 128), 0) % 512, iota((1024, 128), 1)
    pick = jnp.where((r // 128) * 32 + (r % 128) // 4 == lane, 0.0625, 0.0).astype(BF)
    p_ref[...] = mm(acc_ref[...], pick).astype(BF)
    total = jnp.zeros((128, 128), F32)
    for g in range(8):
        total = total + outer_columns(jnp.concatenate([h_ref[g * 8 + k] for k in range(8)], axis=1), g * 8)
    cols_ref[...] = total.astype(BF)


def fine_scratch():
    return [
        pltpu.VMEM((66 * 512, 128), BF),
        pltpu.VMEM((160, 128), BF),
        pltpu.VMEM((160, 128), BF),
    ]


def fine1(at, x, top, bot, cl, cr, w, b):
    return pl.pallas_call(
        fine1_body,
        in_specs=[pl.BlockSpec(memory_space=pltpu.SMEM)] + vm(7),
        out_specs=vm(5),
        out_shape=[
            jax.ShapeDtypeStruct((64, 128, 128), BF),
            jax.ShapeDtypeStruct((512, 128), BF),
            jax.ShapeDtypeStruct((128, 128), BF),
            jax.ShapeDtypeStruct((1056, 128), BF),
            jax.ShapeDtypeStruct((1056, 128), BF),
        ],
        scratch_shapes=fine_scratch() + [pltpu.VMEM((512, 1024), BF)],
        interpret=INTERPRET,
        name="fine1",
    )(at, x, top, bot, cl, cr, w, b)


def fine2_body(at_ref, x_ref, top_ref, bot_ref, cl_ref, cr_ref, w_ref, b_ref, o_ref, s_ref, tl_ref, tr_ref):
    fine_setup(at_ref, top_ref, bot_ref, cl_ref, cr_ref, s_ref, tl_ref, tr_ref)
    bias = bias_rows(b_ref, 128, lambda r: r // 8)

    def finish(i, out):
        v = (out + bias).astype(TERM)
        for k in range(2):
            o_ref[2 * i + k] = v[:, k * 128 : (k + 1) * 128]

    run_conv(lambda z: stage(z, at_ref, x_ref, top_ref, bot_ref, tl_ref, tr_ref, s_ref), finish, w_ref, s_ref)


def fine2(at, x, top, bot, cl, cr, w, b):
    return pl.pallas_call(
        fine2_body,
        in_specs=[pl.BlockSpec(memory_space=pltpu.SMEM)] + vm(7),
        out_specs=vm(1)[0],
        out_shape=jax.ShapeDtypeStruct((64, 128, 128), TERM),
        scratch_shapes=fine_scratch(),
        interpret=INTERPRET,
        name="fine2",
    )(at, x, top, bot, cl, cr, w, b)


def final_body(at_ref, t_ref, c_ref, o_ref):
    r, lane = iota((128, 512), 0), iota((128, 512), 1)
    up = onehot((lane // 128) * 32 + (lane % 128) // 4 == r)
    e = mm(c_ref[...].reshape(128, 128), up).astype(BF)
    rr, kk = iota((128, 32), 0), iota((128, 32), 1)
    widen = onehot((kk % 16 == rr // 8) & (kk // 16 == (rr % 8) // 4))
    both = []
    for p in range(8):
        row = e[p * 16 : p * 16 + 16]
        for k in range(2):
            both.append(
                jnp.concatenate([row[:, k * 256 : k * 256 + 128], row[:, k * 256 + 128 : k * 256 + 256]], axis=0)
            )
    c = mm(widen, jnp.concatenate(both, axis=1))
    for z in range(16):
        v = t_ref[z].astype(F32) + c[:, z * 128 : z * 128 + 128]
        o_ref[:, z] = v.reshape(16, 8, 128).astype(BF)


def final(at, t, c):
    return pl.pallas_call(
        final_body,
        grid_spec=pltpu.PrefetchScalarGridSpec(
            num_scalar_prefetch=1,
            grid=(4,),
            in_specs=[
                pl.BlockSpec((16, 128, 128), lambda i, at: (i, 0, 0)),
                pl.BlockSpec((8, 1, 16, 128), lambda i, at: (i, at[0], 0, 0)),
            ],
            out_specs=pl.BlockSpec((16, 16, 8, 128), lambda i, at: (0, i, 0, 0)),
        ),
        out_shape=jax.ShapeDtypeStruct((16, 64, 8, 128), BF),
        interpret=INTERPRET,
        name="final",
    )(at, t, c)


def spread_x(v):
    lane = iota(v.shape, 1)
    left = jnp.where(lane == 0, jnp.zeros((), BF), pltpu.roll(v, 1, 1))
    right = jnp.where(lane == 127, jnp.zeros((), BF), pltpu.roll(v, 127, 1))
    return jnp.concatenate([left, v, right], axis=0)


def window(s_ref, z, y, rows, per_z):
    both = []
    for k in range(2):
        parts = [
            s_ref[pl.ds(pl.multiple_of((z + dz) * per_z + (y + k) * rows, 16), 3 * rows), :] for dz in range(3)
        ]
        both.append(jnp.concatenate(parts, axis=0))
    return jnp.concatenate(both, axis=1)


def conv1a_body(masked, at_ref, first_ref, second_ref, w_ref, b_ref, o_ref, s_ref):
    swap = at_ref[4] == 1
    reaches = at_ref[5] == 1

    def fill(y, _):
        for zi in range(2):
            a, b = first_ref[zi, y], second_ref[zi, y]
            if masked:
                a = kept(reaches, a)
            for at, v in ((zi, jnp.where(swap, b, a)), (zi + 2, jnp.where(swap, a, b))):
                s_ref[pl.ds(pl.multiple_of(at * 3840 + y * 192, 64), 192), :] = spread_x(v)
        return 0

    lax.fori_loop(0, 20, fill, 0)
    bias = bias_rows(b_ref, 64, lambda r: r)

    def step(i, _):
        outs = [
            mm(w_ref[...], window(s_ref, zo, 6 * i + 2 * k, 192, 3840)) + bias for zo in range(2) for k in range(3)
        ]
        for j in range(6):
            o_ref[j // 3 * 9 + 3 * i + j % 3] = outs[j]
        return 0

    lax.fori_loop(0, 3, step, 0)


def conv1a(at, first, second, w, b, name):
    return pl.pallas_call(
        functools.partial(conv1a_body, name == "distant"),
        in_specs=[pl.BlockSpec(memory_space=pltpu.SMEM)] + vm(4),
        out_specs=vm(1)[0],
        out_shape=jax.ShapeDtypeStruct((18, 64, 256), F32),
        scratch_shapes=[pltpu.VMEM((4 * 20 * 192, 128), BF)],
        interpret=INTERPRET,
    )(at, first, second, w, b)


def coarse_body(at_ref, got_ref, near_ref, far_ref, w1_ref, w2_ref, b_ref, proj_ref, out_ref, ctx_ref, sp_ref, sm_ref, co_ref, ct_ref):
    n, w = at_ref[2], at_ref[3]
    odd = at_ref[4] == 1
    r, c = iota((512, 512), 0), iota((512, 512), 1)
    order = onehot((r % 128 // 32 == c // 128) & (r // 128 == c % 128 // 32) & (r % 32 == c % 32))
    for wb in range(10):
        if wb == 0:
            blocks = [kept(n > 0, got_ref[8 * k + 7, 1]) for k in range(4)]
        elif wb == 9:
            blocks = [kept(n < 3, got_ref[8 * k, 1]) for k in range(4)]
        else:
            blocks = [got_ref[8 * k + wb - 1, 0] for k in range(4)]
        t = mm(jnp.concatenate(blocks, axis=1), order).astype(BF)
        for s in range(3):
            for zi in range(4):
                v = t[s * 16 : s * 16 + 16, zi * 128 : zi * 128 + 128]
                base = (2 * s + zi // 2) * 960 + (2 * wb + zi % 2) * 48
                sp_ref[base : base + 48, :] = spread_x(v)

    def mid(yp, _):
        outs = []
        for zo in range(4):
            i = zo % 2 * 9 + yp
            low, high = (far_ref, near_ref) if zo < 2 else (near_ref, far_ref)
            part = jnp.where(odd, high[i], low[i])
            outs.append(mm(w1_ref[...], window(sp_ref, zo, 2 * yp, 48, 960)) + part)
        keep = [(yp > 0) | (n > 0), (yp < 8) | (n < 3)]
        for zo in range(4):
            v = jnp.maximum(outs[zo], 0.0)
            for k in range(2):
                inside = keep[k] & (w > 0) if zo == 0 else keep[k] & (w < 31) if zo == 3 else keep[k]
                m = jnp.where(inside, v[:, k * 128 : k * 128 + 128], 0.0).astype(BF)
                sm_ref[pl.ds(pl.multiple_of(zo * 3456 + (2 * yp + k) * 192, 64), 192), :] = spread_x(m)
        return 0

    lax.fori_loop(0, 9, mid, 0)
    bias = bias_rows(b_ref, 64, lambda r: r)
    proj = proj_ref[...]

    def last(i, _):
        outs = [mm(w2_ref[...], window(sm_ref, z, 4 * i + 2 * h, 192, 3456)) for z in range(2) for h in range(2)]
        for j in range(4):
            z, b = j // 2, 2 * i + j % 2
            o = jnp.maximum(outs[j] + bias, 0.0).astype(BF)
            ct = mm(proj, o).astype(BF)
            for k in range(2):
                lanes = slice(k * 128, k * 128 + 128)
                co_ref[pl.ds(pl.multiple_of((2 * b + k) * 64, 64), 64), z * 128 : z * 128 + 128] = o[:, lanes]
                at = (z * 2 + k) * 128
                ct_ref[pl.ds(pl.multiple_of(b * 16, 16), 16), at : at + 128] = ct[:, lanes]
        return 0

    lax.fori_loop(0, 4, last, 0)
    back = onehot((c % 128 // 32 == r // 128) & (c // 128 == r % 128 // 32) & (r % 32 == c % 32))
    ct = mm(ct_ref[...], back).astype(BF)
    for b in range(8):
        for k in range(4):
            block = ct[b * 16 : b * 16 + 16, k * 128 : k * 128 + 128]
            for to in range(4):
                ctx_ref[to, b, k] = jnp.where(n == to, block, jnp.zeros((), BF))
    r, k = iota((256, 256), 0), iota((256, 256), 1)
    perm = onehot((r % 16) * 16 + r // 16 == k)
    for g in range(4):
        rows = jnp.concatenate([co_ref[y * 64 + g * 16 : y * 64 + g * 16 + 16, :] for y in range(16)], axis=0)
        o = mm(perm, rows).astype(BF)
        for z in range(2):
            out_ref[g * 16 : g * 16 + 16, z] = o[:, z * 128 : z * 128 + 128].reshape(16, 16, 128)


def coarse(at, got, near, far, w1, w2, b2, proj):
    def whole(shape):
        return pl.BlockSpec(shape, lambda i, at: (0,) * len(shape))

    return pl.pallas_call(
        coarse_body,
        grid_spec=pltpu.PrefetchScalarGridSpec(
            num_scalar_prefetch=1,
            grid=(1,),
            in_specs=[
                whole((32, 2, 48, 128)),
                whole((18, 64, 256)),
                whole((18, 64, 256)),
                whole((64, 432)),
                whole((64, 1728)),
                whole((1, 64)),
                whole((16, 64)),
            ],
            out_specs=[whole((64, 2, 16, 128)), whole((4, 8, 4, 16, 128))],
            scratch_shapes=[
                pltpu.VMEM((6 * 20 * 48, 128), BF),
                pltpu.VMEM((4 * 18 * 192, 128), BF),
                pltpu.VMEM((1024, 256), BF),
                pltpu.VMEM((128, 512), BF),
            ],
        ),
        out_shape=[
            jax.ShapeDtypeStruct((64, 2, 16, 128), BF),
            jax.ShapeDtypeStruct((4, 8, 4, 16, 128), BF),
        ],
        interpret=INTERPRET,
        name="coarse",
    )(at, got, near, far, w1, w2, b2, proj)


def shift(array, axis, by):
    count = lax.axis_size(axis)
    return lax.ppermute(array, axis, [(i, (i + by) % count) for i in range(count)])


def across_y(down, up, from_left, from_right):
    down = lax.dynamic_update_slice(down, jnp.concatenate([from_left[112:128], from_right[112:128]]), (1024, 0))
    up = lax.dynamic_update_slice(up, jnp.concatenate([from_left[0:16], from_right[0:16]]), (1024, 0))
    return shift(down, "wide", 1), shift(up, "wide", -1)


def turns(by):
    pairs = []
    for a in range(4):
        for b in range(8):
            to = (a + by * ((b == 7) - (b == 0))) % 4
            pairs += [((8 * a + b) * 4 + n, (8 * n + b) * 4 + to) for n in range(4)]
    return pairs


def taps(w):
    return jnp.transpose(w, (2, 3, 4, 0, 1)).reshape(27, w.shape[0], w.shape[1])


def local(
    fine_in,
    coarse_in,
    w_fine1,
    b_fine1,
    w_fine2,
    b_fine2,
    w_coarse1,
    b_coarse1,
    w_coarse2,
    b_coarse2,
    w_proj,
):
    w = lax.axis_index("wide")
    n = lax.axis_index("narrow")
    reaches = jnp.where(w % 2 == 1, w < 31, w > 0).astype(jnp.int32)
    at = jnp.stack([w // 8, w % 8, n, w, w % 2, reaches])
    rows, down, up, cols = prep(fine_in)
    ct, east, west = cprep(coarse_in, cols)
    from_left = shift(east, "narrow", 1)
    from_right = shift(west, "narrow", -1)
    top, bottom = across_y(down, up, from_left, from_right)
    wf1, wf2, wa, wb, wc = weights(taps(w_fine1), taps(w_fine2), taps(w_coarse1), taps(w_coarse2))
    slab = jnp.concatenate(
        [
            jnp.where(n > 0, from_left[128:], jnp.zeros((), BF)).reshape(2, 2, 64, 128),
            ct,
            jnp.where(n < 3, from_right[128:], jnp.zeros((), BF)).reshape(2, 2, 64, 128),
        ],
        axis=1,
    )
    mate = lax.ppermute(slab, "wide", [(i, i ^ 1) for i in range(32)])
    hops = [(i, i + 2 - 4 * (i % 2)) for i in range(32)]
    far = lax.ppermute(mate, "wide", [(i, j % 32) for i, j in hops])
    hidden, pooled, hcols, hdown, hup = fine1(
        at, rows, top, bottom, from_left, from_right, wf1, b_fine1[None]
    )
    turned = lax.ppermute(pooled, ("wide", "narrow"), turns(0))
    ends = lax.ppermute(pooled, ("wide", "narrow"), turns(1))
    slabs = jnp.stack([turned, ends]).reshape(2, 32, 16, 128)
    slabs = jnp.pad(slabs, ((0, 0), (1, 1), (0, 0), (0, 0)))
    parcels = jnp.stack([slabs[:, j : j + 32] for j in range(3)], axis=2).transpose(1, 0, 2, 3, 4)
    got = lax.all_to_all(parcels.reshape(32, 96, 128), "wide", 0, 0, tiled=True)
    near_part = conv1a(at, slab, mate, wa, b_coarse1[None], "near")
    hleft = shift(hcols, "narrow", 1)
    hright = shift(hcols, "narrow", -1)
    htop, hbottom = across_y(hdown, hup, hleft, hright)
    far_part = conv1a(at, far, slab, wa, b_coarse1[None], "distant")
    coarse_out, context = coarse(at, got.reshape(32, 2, 48, 128), near_part, far_part, wb, wc, b_coarse2[None], w_proj)
    arrived = lax.all_to_all(context.reshape(128, 16, 128), ("wide", "narrow"), 0, 0, tiled=True)
    term = fine2(at, hidden, htop, hbottom, hleft, hright, wf2, b_fine2[None])
    fine_out = final(at, term, arrived.reshape(32, 4, 16, 128))
    return fine_out, coarse_out


def solution(mesh):
    return jax.shard_map(
        local,
        mesh=mesh,
        in_specs=(P(None, None, "wide", "narrow"), P(None, "wide", "narrow", None)) + (P(),) * 9,
        out_specs=(P(None, None, "wide", "narrow"), P(None, "wide", "narrow", None)),
        check_vma=False,
    )
```

time: 172 us -> 163 us (0.948)
  waiting for transfers between devices: 55.9 us -> 41.1 us
  Pallas kernels: 59.7 us -> 66.7 us
  local copies, waits for them, and re-layouts: 7.9 us -> 5.67 us
    ppermute x1, waiting for transfers between devices: 26 us -> 6.23 us  [local(): mate = lax.ppermute(slab, 'wide', [(i, i ^ 1) for i in range(32)])]
    ppermute x0 -> x2, starting transfers between devices: none -> 8.96 us  [the longest x1 7.04 us: local(): ends = lax.ppermute(pooled, ('wide', 'narrow'), turns(1))]
    pallas_call x2 -> x4, Pallas kernels: 13 us -> 20.6 us  [the longest x1 9.98 us: fine2(): pl.pallas_call(fine2_body, in_specs=[pl.BlockSpec(memory_space=pltpu.SMEM...]
    ppermute x0 -> x2, waiting for transfers between devices: none -> 4.66 us  [the longest x1 3.84 us: local(): turned = lax.ppermute(pooled, ('wide', 'narrow'), turns(0))]
    all_to_all x1, starting transfers between devices: 13.8 us -> 10.3 us  [local(): got = lax.all_to_all(parcels.reshape(32, 96, 128), 'wide', 0, 0, tiled=True)]
    slice x3 -> x0, local copies, waits for them, and re-layouts: 3.03 us -> none  [the longest x2 2.15 us: across_y(): rows[:, 0:16, :].reshape(1024, 128)]
    ppermute x8, waiting for transfers between devices: 20.1 us -> 22.7 us  [shift(): lax.ppermute(array, axis, [(i, (i + by) % count) for i in range(count)])]
    ppermute x1, waiting for transfers between devices: 9.73 us -> 7.48 us  [local(): far = lax.ppermute(mate, 'wide', [(i, j % 32) for i, j in hops])]
  transfers between devices with their start and end apart: 12 -> 14, of which waited for: 8 -> 9; matrix products, arithmetic and copies ran while one was open for 3% -> 2% of each run, Pallas kernels for 9% -> 26%
where the time goes in v1:
time: 163 us
  Pallas kernels  66.7 us (41%)
  starting transfers between devices  46.8 us (29%)
  waiting for transfers between devices  41.1 us (25%)
  local copies, waits for them, and re-layouts  5.67 us (3%)
    ppermute x8, waiting for transfers between devices, shift(): lax.ppermute(array, axis, [(i, (i + by) % count) for i in range(count)])  22.7 us
    ppermute x8, starting transfers between devices, shift(): lax.ppermute(array, axis, [(i, (i + by) % count) for i in range(count)])  20.9 us
    pallas_call x2, Pallas kernels, conv1a(): pl.pallas_call(functools.partial(conv1a_body, name == 'distant'), in_spec...  15.4 us
    pallas_call x1, Pallas kernels, coarse(): pl.pallas_call(coarse_body, grid_spec=pltpu.PrefetchScalarGridSpec(num_sc...  13.9 us
    pallas_call x1, Pallas kernels, fine1(): pl.pallas_call(fine1_body, in_specs=[pl.BlockSpec(memory_space=pltpu.SMEM...  10.6 us
    all_to_all x1, starting transfers between devices, local(): got = lax.all_to_all(parcels.reshape(32, 96, 128), 'wide', 0, 0, tiled=True)  10.3 us
    pallas_call x1, Pallas kernels, fine2(): pl.pallas_call(fine2_body, in_specs=[pl.BlockSpec(memory_space=pltpu.SMEM...  9.98 us
    ppermute x1, waiting for transfers between devices, local(): far = lax.ppermute(mate, 'wide', [(i, j % 32) for i, j in hops])  7.48 us
  transfers between devices with their start and end apart: 14, of which 9 were waited for; matrix products, arithmetic and copies ran while one was open for 2% of the time, Pallas kernels for 26%

profile of v1, /device:TPU:1, one launch (start us, length us, event | category | flops | bytes accessed | tf_op | source)
XLA Modules:
  0.0 162.6 jit_solution(15593000931391120250)
XLA Ops:
  0.6 6.3 %prep.1 = (bf16[64,128,128]{2,1,0:T(8,128)(2,1)}, bf16[1056,128]{1,0:T(8,128)(2,1)}, bf16[1056,128]{1,0:T(8,128)(2,1)}, bf16[128,128]{1,0:T(8,128)(2,1)}) custom-call(bf16[16,64,8,128]{3,2,1,0:T(8,128)(2,1)} %x_ref.2), custom_call_target="tpu_custom_call" | custom-call | tf_op jit(solution)/shard_map/prep/pallas_call | solution.py:70
  6.9 2.2 %cprep.1 = (bf16[2,16,64,128]{3,2,1,0:T(8,128)(2,1)}, bf16[384,128]{1,0:T(8,128)(2,1)}, bf16[384,128]{1,0:T(8,128)(2,1)}) custom-call(bf16[64,2,16,128]{3,2,1,0:T(8,128)(2,1)} %x_ref.3, bf16[128,128]{1,0:T(8,128)(2,1)} %get-tuple-element.23.cols_ref), custom_call_target="tpu_custom_call" | custom-call | tf_op jit(solution)/shard_map/cprep/pallas_call | solution.py:114
  9.1 1.4 collective-permute-start.1
  10.5 2.9 %collective-permute-start = (bf16[384,128]{1,0:T(8,128)(2,1)}, bf16[384,128]{1,0:T(8,128)(2,1)S(1)}, u32[]{:S(2)}, u32[]{:S(2)}) collective-permute-start(bf16[384,128]{1,0:T(8,128)(2,1)} %get-tuple-element.24), channel_id=1, source_target_pairs={{0,1},{1,2},{2,3},{3,0},{4,5},{5,6},{6,7},{7,4},{8,9},{9,10},{10,1... | collective-permute-start | bytes 294920 | tf_op jit(solution)/shard_map/ppermute | solution.py:512
  13.4 3.2 %weights.1 = (bf16[128,1536]{1,0:T(8,128)(2,1)}, bf16[128,1536]{1,0:T(8,128)(2,1)}, bf16[64,1728]{1,0:T(8,128)(2,1)}, bf16[64,432]{1,0:T(8,128)(2,1)}, bf16[64,1728]{1,0:T(8,128)(2,1)}) custom-call(bf16[27,16,16]{2,1,0:T(8,128)(2,1)} %bitcast.51, bf16[27,16,16]{2,1,0:T(8,128)(2,1)} %bitcast.52, bf16[27,64,80]{2,1,0:T(8,128)(2,1)} %bitcast.47, ...), custom_call_target="tpu_custom_call" | custom-call | tf_op jit(solution)/shard_map/weights/pallas_call | solution.py:148
  17.9 1.1 collective-permute-start.2
  19.5 5.7 %collective-permute-start.3 = (bf16[1056,128]{1,0:T(8,128)(2,1)}, bf16[1056,128]{1,0:T(8,128)(2,1)S(1)}, u32[]{:S(2)}, u32[]{:S(2)}) collective-permute-start(bf16[1056,128]{1,0:T(8,128)(2,1)} %maximum_dynamic-update-slice_fusion.1), channel_id=1, source_target_pairs={{0,124},{4,0},{8,4},{12,8},{16,12},{20,16},{24,20},{28,24},{32,28}... | collective-permute-start | bytes 811016 | tf_op jit(solution)/shard_map/ppermute | solution.py:512
  25.2 5.4 %collective-permute-done.2.top_ref = bf16[1056,128]{1,0:T(8,128)(2,1)S(1)} collective-permute-done((bf16[1056,128]{1,0:T(8,128)(2,1)}, bf16[1056,128]{1,0:T(8,128)(2,1)S(1)}, u32[]{:S(2)}, u32[]{:S(2)}) %collective-permute-start.2) | collective-permute-done | bytes 270368 | tf_op jit(solution)/shard_map/ppermute | solution.py:512
  30.6 0.9 collective-permute-done.3.bot_ref
  32.2 10.6 %fine1.1 = (bf16[64,128,128]{2,1,0:T(8,128)(2,1)}, bf16[512,128]{1,0:T(8,128)(2,1)}, bf16[128,128]{1,0:T(8,128)(2,1)}, bf16[1056,128]{1,0:T(8,128)(2,1)}, bf16[1056,128]{1,0:T(8,128)(2,1)}) custom-call(s32[6]{0:T(128)} %stack.56.at_ref, bf16[64,128,128]{2,1,0:T(8,128)(2,1)} %get-tuple-element.21.x_ref, bf16[1056,128]{1,0:T(8,128)(2,1)} %copy-done.8, ...), custom_call_target="tpu_custom_call" | custom-call | tf_op jit(solution)/shard_map/fine1/pallas_call | solution.py:273
  42.8 7.0 %collective-permute-start.9 = (bf16[512,128]{1,0:T(8,128)(2,1)}, bf16[512,128]{1,0:T(8,128)(2,1)S(1)}, u32[]{:S(2)}, u32[]{:S(2)}) collective-permute-start(bf16[512,128]{1,0:T(8,128)(2,1)} %get-tuple-element.33), channel_id=1, source_target_pairs={{0,3},{1,35},{2,67},{3,99},{4,4},{5,36},{6,68},{7,100},{8,8},{9,40... | collective-permute-start | bytes 393224 | tf_op jit(solution)/shard_map/ppermute | solution.py:572
  49.9 1.9 %collective-permute-start.8 = (bf16[512,128]{1,0:T(8,128)(2,1)}, bf16[512,128]{1,0:T(8,128)(2,1)S(1)}, u32[]{:S(2)}, u32[]{:S(2)}) collective-permute-start(bf16[512,128]{1,0:T(8,128)(2,1)} %get-tuple-element.33), channel_id=1, source_target_pairs={{0,0},{1,32},{2,64},{3,96},{4,4},{5,36},{6,68},{7,100},{8,8},{9,40... | collective-permute-start | bytes 393224 | tf_op jit(solution)/shard_map/ppermute | solution.py:571
  52.0 0.8 collective-permute-done.9
  52.8 3.8 %collective-permute-done.8 = bf16[512,128]{1,0:T(8,128)(2,1)S(1)} collective-permute-done((bf16[512,128]{1,0:T(8,128)(2,1)}, bf16[512,128]{1,0:T(8,128)(2,1)S(1)}, u32[]{:S(2)}, u32[]{:S(2)}) %collective-permute-start.8) | collective-permute-done | bytes 131104 | tf_op jit(solution)/shard_map/ppermute | solution.py:571
  56.9 1.0 copy.14
  57.9 10.3 %all-to-all-start = ((bf16[32,96,128]{2,1,0:T(8,128)(2,1)}), bf16[32,96,128]{2,1,0:T(8,128)(2,1)S(1)}, u32[]{:S(2)}, u32[]{:S(2)}) async-start(bf16[32,96,128]{2,1,0:T(8,128)(2,1)} %bitcast.24), calls=%async_computation | async-start | bytes 1572864 | tf_op jit(solution)/shard_map/all_to_all | solution.py:576
  68.2 6.2 %collective-permute-done.10.second_ref = bf16[2,20,64,128]{3,2,1,0:T(8,128)(2,1)S(1)} collective-permute-done((bf16[2,20,64,128]{3,2,1,0:T(8,128)(2,1)S(1)}, bf16[2,20,64,128]{3,2,1,0:T(8,128)(2,1)S(1)}, u32[]{:S(2)}, u32[]{:S(2)}) %collective-permute-start.10) | collective-permute-done | bytes 655392 | tf_op jit(solution)/shard_map/ppermute | solution.py:565
  74.9 2.9 %collective-permute-start.4 = (bf16[128,128]{1,0:T(8,128)(2,1)S(1)}, bf16[128,128]{1,0:T(8,128)(2,1)S(1)}, u32[]{:S(2)}, u32[]{:S(2)}) collective-permute-start(bf16[128,128]{1,0:T(8,128)(2,1)S(1)} %copy-done.16), channel_id=1, source_target_pairs={{0,1},{1,2},{2,3},{3,0},{4,5},{5,6},{6,7},{7,4},{8,9},{9,10},{10,1... | collective-permute-start | bytes 98312 | tf_op jit(solution)/shard_map/ppermute | solution.py:512
  77.8 3.2 %collective-permute-done.5.cr_ref = bf16[128,128]{1,0:T(8,128)(2,1)S(1)} collective-permute-done((bf16[128,128]{1,0:T(8,128)(2,1)S(1)}, bf16[128,128]{1,0:T(8,128)(2,1)S(1)}, u32[]{:S(2)}, u32[]{:S(2)}) %collective-permute-start.5) | collective-permute-done | bytes 32800 | tf_op jit(solution)/shard_map/ppermute | solution.py:512
  81.1 7.7 %shard_map.122.near_ref = f32[18,64,256]{2,1,0:T(8,128)} custom-call(s32[6]{0:T(128)} %stack.56.at_ref, bf16[2,20,64,128]{3,2,1,0:T(8,128)(2,1)} %copy-done, bf16[2,20,64,128]{3,2,1,0:T(8,128)(2,1)} %copy-done.3, bf16[64,1728]{1,0:T(8,128)(2,1)} %get-tuple-element.35.w_ref, f32[1,64]{1,0:T(1,128)} %bitcast.53), custom_call_target="tpu_custom_call" | custom-call | tf_op jit(solution)/shard_map/pallas_call | solution.py:396
  88.7 7.5 %collective-permute-done.11.first_ref = bf16[2,20,64,128]{3,2,1,0:T(8,128)(2,1)S(1)} collective-permute-done((bf16[2,20,64,128]{3,2,1,0:T(8,128)(2,1)S(1)}, bf16[2,20,64,128]{3,2,1,0:T(8,128)(2,1)S(1)}, u32[]{:S(2)}, u32[]{:S(2)}) %collective-permute-start.11) | collective-permute-done | bytes 655392 | tf_op jit(solution)/shard_map/ppermute | solution.py:567
  96.2 0.9 copy-done.4
  97.1 7.7 %shard_map.123.far_ref = f32[18,64,256]{2,1,0:T(8,128)} custom-call(s32[6]{0:T(128)} %stack.56.at_ref, bf16[2,20,64,128]{3,2,1,0:T(8,128)(2,1)} %copy-done.4, bf16[2,20,64,128]{3,2,1,0:T(8,128)(2,1)} %copy-done, bf16[64,1728]{1,0:T(8,128)(2,1)} %get-tuple-element.35.w_ref, f32[1,64]{1,0:T(1,128)} %bitcast.54), custom_call_target="tpu_custom_call" | custom-call | tf_op jit(solution)/shard_map/pallas_call | solution.py:396
  104.8 0.9 copy-done.1
  105.7 13.9 %coarse.1 = (bf16[64,2,16,128]{3,2,1,0:T(8,128)(2,1)}, bf16[4,8,4,16,128]{4,3,2,1,0:T(8,128)(2,1)}) custom-call(s32[6]{0:T(128)} %stack.56.at_ref, bf16[32,2,48,128]{3,2,1,0:T(8,128)(2,1)} %bitcast.40, f32[18,64,256]{2,1,0:T(8,128)} %shard_map.122.near_ref, f32[18,64,256]{2,1,0:T(8,128)} %shard_map.123.far_ref, bf16[64,432]{1,0:T(8,128)(2,1)} %get-tuple-element.36.w1_ref, ...), custom_call_target="tpu_custom_call" | custom-call | tf_op jit(solution)/shard_map/coarse/pallas_call | solution.py:479
  119.6 6.5 %all-to-all-start.1 = ((bf16[128,16,128]{2,1,0:T(8,128)(2,1)}), bf16[128,16,128]{2,1,0:T(8,128)(2,1)S(1)}, u32[]{:S(2)}, u32[]{:S(2)}) async-start(bf16[128,16,128]{2,1,0:T(8,128)(2,1)} %bitcast.42), calls=%async_computation.1 | async-start | bytes 1048576 | tf_op jit(solution)/shard_map/all_to_all | solution.py:583
  126.2 1.4 collective-permute-start.6
  127.6 5.1 %collective-permute-start.7 = (bf16[1056,128]{1,0:T(8,128)(2,1)S(1)}, bf16[1056,128]{1,0:T(8,128)(2,1)S(1)}, u32[]{:S(2)}, u32[]{:S(2)}) collective-permute-start(bf16[1056,128]{1,0:T(8,128)(2,1)S(1)} %maximum_dynamic-update-slice_fusion.3), channel_id=1, source_target_pairs={{0,124},{4,0},{8,4},{12,8},{16,12},{20,16},{24,20},{28,24},{32,28}... | collective-permute-start | bytes 811016 | tf_op jit(solution)/shard_map/ppermute | solution.py:512
  132.7 11.6 %collective-permute-done.6.top_ref = bf16[1056,128]{1,0:T(8,128)(2,1)S(1)} collective-permute-done((bf16[1056,128]{1,0:T(8,128)(2,1)S(1)}, bf16[1056,128]{1,0:T(8,128)(2,1)S(1)}, u32[]{:S(2)}, u32[]{:S(2)}) %collective-permute-start.6) | collective-permute-done | bytes 270368 | tf_op jit(solution)/shard_map/ppermute | solution.py:512
  144.3 1.6 %collective-permute-done.7.bot_ref = bf16[1056,128]{1,0:T(8,128)(2,1)S(1)} collective-permute-done((bf16[1056,128]{1,0:T(8,128)(2,1)S(1)}, bf16[1056,128]{1,0:T(8,128)(2,1)S(1)}, u32[]{:S(2)}, u32[]{:S(2)}) %collective-permute-start.7) | collective-permute-done | bytes 270368 | tf_op jit(solution)/shard_map/ppermute | solution.py:512
  146.6 10.0 %fine2.1.t_ref = bf16[64,128,128]{2,1,0:T(8,128)(2,1)} custom-call(s32[6]{0:T(128)} %stack.56.at_ref, bf16[64,128,128]{2,1,0:T(8,128)(2,1)} %get-tuple-element.28.x_ref, bf16[1056,128]{1,0:T(8,128)(2,1)} %copy-done.9, bf16[1056,128]{1,0:T(8,128)(2,1)} %copy-done.11, bf16[128,128]{1,0:T(8,128)(2,1)} %copy-done.13, bf16[128,128]{1,0:T(8,128)(2,1)} %copy-done.12, ...), custom_call_target="tpu_custom_call" | custom-call | tf_op jit(solution)/shard_map/fine2/pallas_call | solution.py:303
  157.4 5.2 %final.1 = bf16[16,64,8,128]{3,2,1,0:T(8,128)(2,1)} custom-call(s32[6]{0:T(128)} %stack.56.at_ref, bf16[64,128,128]{2,1,0:T(8,128)(2,1)} %fine2.1.t_ref, bf16[32,4,16,128]{3,2,1,0:T(8,128)(2,1)} %bitcast.41), custom_call_target="tpu_custom_call" | custom-call | tf_op jit(solution)/shard_map/final/pallas_call | solution.py:334
  (55 shorter events, 5.0 us)
Async XLA Ops:
  9.1 8.0 %collective-permute-start.1 = (bf16[384,128]{1,0:T(8,128)(2,1)}, bf16[384,128]{1,0:T(8,128)(2,1)S(1)}, u32[]{:S(2)}, u32[]{:S(2)}) collective-permute-start(bf16[384,128]{1,0:T(8,128)(2,1)} %get-tuple-element.25), channel_id=1, source_target_pairs={{0,3},{1,0},{2,1},{3,2},{4,7},{5,4},{6,5},{7,6},{8,11},{9,8},{10,9... | collective-permute-start | bytes 294920 | tf_op jit(solution)/shard_map/ppermute | solution.py:512
  10.5 6.7 %collective-permute-start = (bf16[384,128]{1,0:T(8,128)(2,1)}, bf16[384,128]{1,0:T(8,128)(2,1)S(1)}, u32[]{:S(2)}, u32[]{:S(2)}) collective-permute-start(bf16[384,128]{1,0:T(8,128)(2,1)} %get-tuple-element.24), channel_id=1, source_target_pairs={{0,1},{1,2},{2,3},{3,0},{4,5},{5,6},{6,7},{7,4},{8,9},{9,10},{10,1... | collective-permute-start | bytes 294920 | tf_op jit(solution)/shard_map/ppermute | solution.py:512
  13.4 38.4 %copy-start.5 = (bf16[2,16,64,128]{3,2,1,0:T(8,128)(2,1)S(1)}, bf16[2,16,64,128]{3,2,1,0:T(8,128)(2,1)}, u32[]{:S(2)}) copy-start(bf16[2,16,64,128]{3,2,1,0:T(8,128)(2,1)} %get-tuple-element.34) | copy-start | bytes 1572868
  17.1 14.4 %copy-start.6 = (bf16[384,128]{1,0:T(8,128)(2,1)}, bf16[384,128]{1,0:T(8,128)(2,1)S(1)}, u32[]{:S(2)}) copy-start(bf16[384,128]{1,0:T(8,128)(2,1)S(1)} %collective-permute-done.1.cr_ref) | copy-start | bytes 294916
  17.1 14.4 %copy-start.7 = (bf16[384,128]{1,0:T(8,128)(2,1)}, bf16[384,128]{1,0:T(8,128)(2,1)S(1)}, u32[]{:S(2)}) copy-start(bf16[384,128]{1,0:T(8,128)(2,1)S(1)} %collective-permute-done.cl_ref) | copy-start | bytes 294916
  17.9 12.8 %collective-permute-start.2 = (bf16[1056,128]{1,0:T(8,128)(2,1)}, bf16[1056,128]{1,0:T(8,128)(2,1)S(1)}, u32[]{:S(2)}, u32[]{:S(2)}) collective-permute-start(bf16[1056,128]{1,0:T(8,128)(2,1)} %maximum_dynamic-update-slice_fusion), channel_id=1, source_target_pairs={{0,4},{4,8},{8,12},{12,16},{16,20},{20,24},{24,28},{28,32},{32,36}... | collective-permute-start | bytes 811016 | tf_op jit(solution)/shard_map/ppermute | solution.py:512
  19.5 12.0 %collective-permute-start.3 = (bf16[1056,128]{1,0:T(8,128)(2,1)}, bf16[1056,128]{1,0:T(8,128)(2,1)S(1)}, u32[]{:S(2)}, u32[]{:S(2)}) collective-permute-start(bf16[1056,128]{1,0:T(8,128)(2,1)} %maximum_dynamic-update-slice_fusion.1), channel_id=1, source_target_pairs={{0,124},{4,0},{8,4},{12,8},{16,12},{20,16},{24,20},{28,24},{32,28}... | collective-permute-start | bytes 811016 | tf_op jit(solution)/shard_map/ppermute | solution.py:512
  30.6 0.9 copy-start.8
  31.5 0.7 copy-start.10
  42.8 10.0 %collective-permute-start.9 = (bf16[512,128]{1,0:T(8,128)(2,1)}, bf16[512,128]{1,0:T(8,128)(2,1)S(1)}, u32[]{:S(2)}, u32[]{:S(2)}) collective-permute-start(bf16[512,128]{1,0:T(8,128)(2,1)} %get-tuple-element.33), channel_id=1, source_target_pairs={{0,3},{1,35},{2,67},{3,99},{4,4},{5,36},{6,68},{7,100},{8,8},{9,40... | collective-permute-start | bytes 393224 | tf_op jit(solution)/shard_map/ppermute | solution.py:572
  49.9 6.8 %collective-permute-start.8 = (bf16[512,128]{1,0:T(8,128)(2,1)}, bf16[512,128]{1,0:T(8,128)(2,1)S(1)}, u32[]{:S(2)}, u32[]{:S(2)}) collective-permute-start(bf16[512,128]{1,0:T(8,128)(2,1)} %get-tuple-element.33), channel_id=1, source_target_pairs={{0,0},{1,32},{2,64},{3,96},{4,4},{5,36},{6,68},{7,100},{8,8},{9,40... | collective-permute-start | bytes 393224 | tf_op jit(solution)/shard_map/ppermute | solution.py:571
  51.9 6.0 %copy-start = (bf16[2,20,64,128]{3,2,1,0:T(8,128)(2,1)}, bf16[2,20,64,128]{3,2,1,0:T(8,128)(2,1)S(1)}, u32[]{:S(2)}) copy-start(bf16[2,20,64,128]{3,2,1,0:T(8,128)(2,1)S(1)} %pad_maximum_fusion.first_ref.second_ref) | copy-start | bytes 1966084
  51.9 22.6 %collective-permute-start.10 = (bf16[2,20,64,128]{3,2,1,0:T(8,128)(2,1)S(1)}, bf16[2,20,64,128]{3,2,1,0:T(8,128)(2,1)S(1)}, u32[]{:S(2)}, u32[]{:S(2)}) collective-permute-start(bf16[2,20,64,128]{3,2,1,0:T(8,128)(2,1)S(1)} %pad_maximum_fusion.first_ref.second_ref), channel_id=1, source_target_pairs={{0,4},{4,0},{8,12},{12,8},{16,20},{20,16},{24,28},{28,24},{32,36},... | collective-permute-start | bytes 1966088 | tf_op jit(solution)/shard_map/ppermute | solution.py:565
  56.8 17.7 %copy-start.16 = (bf16[128,128]{1,0:T(8,128)(2,1)S(1)}, bf16[128,128]{1,0:T(8,128)(2,1)}, u32[]{:S(2)}) copy-start(bf16[128,128]{1,0:T(8,128)(2,1)} %get-tuple-element.30) | copy-start | bytes 98308
  57.9 46.9 %all-to-all-start = ((bf16[32,96,128]{2,1,0:T(8,128)(2,1)}), bf16[32,96,128]{2,1,0:T(8,128)(2,1)S(1)}, u32[]{:S(2)}, u32[]{:S(2)}) async-start(bf16[32,96,128]{2,1,0:T(8,128)(2,1)} %bitcast.24), calls=%async_computation | async-start | bytes 1572864 | tf_op jit(solution)/shard_map/all_to_all | solution.py:576
  74.5 6.6 %copy-start.3 = (bf16[2,20,64,128]{3,2,1,0:T(8,128)(2,1)}, bf16[2,20,64,128]{3,2,1,0:T(8,128)(2,1)S(1)}, u32[]{:S(2)}) copy-start(bf16[2,20,64,128]{3,2,1,0:T(8,128)(2,1)S(1)} %collective-permute-done.10.second_ref) | copy-start | bytes 1966084
  74.5 21.8 %collective-permute-start.11 = (bf16[2,20,64,128]{3,2,1,0:T(8,128)(2,1)S(1)}, bf16[2,20,64,128]{3,2,1,0:T(8,128)(2,1)S(1)}, u32[]{:S(2)}, u32[]{:S(2)}) collective-permute-start(bf16[2,20,64,128]{3,2,1,0:T(8,128)(2,1)S(1)} %collective-permute-done.10.second_ref), channel_id=1, source_target_pairs={{0,8},{4,124},{8,16},{12,4},{16,24},{20,12},{24,32},{28,20},{32,40... | collective-permute-start | bytes 1966088 | tf_op jit(solution)/shard_map/ppermute | solution.py:567
  74.5 6.6 %collective-permute-start.5 = (bf16[128,128]{1,0:T(8,128)(2,1)S(1)}, bf16[128,128]{1,0:T(8,128)(2,1)S(1)}, u32[]{:S(2)}, u32[]{:S(2)}) collective-permute-start(bf16[128,128]{1,0:T(8,128)(2,1)S(1)} %copy-done.16), channel_id=1, source_target_pairs={{0,3},{1,0},{2,1},{3,2},{4,7},{5,4},{6,5},{7,6},{8,11},{9,8},{10,9... | collective-permute-start | bytes 98312 | tf_op jit(solution)/shard_map/ppermute | solution.py:512
  74.9 51.2 %collective-permute-start.4 = (bf16[128,128]{1,0:T(8,128)(2,1)S(1)}, bf16[128,128]{1,0:T(8,128)(2,1)S(1)}, u32[]{:S(2)}, u32[]{:S(2)}) collective-permute-start(bf16[128,128]{1,0:T(8,128)(2,1)S(1)} %copy-done.16), channel_id=1, source_target_pairs={{0,1},{1,2},{2,3},{3,0},{4,5},{5,6},{6,7},{7,4},{8,9},{9,10},{10,1... | collective-permute-start | bytes 98312 | tf_op jit(solution)/shard_map/ppermute | solution.py:512
  81.0 23.8 %copy-start.12 = (bf16[128,128]{1,0:T(8,128)(2,1)}, bf16[128,128]{1,0:T(8,128)(2,1)S(1)}, u32[]{:S(2)}) copy-start(bf16[128,128]{1,0:T(8,128)(2,1)S(1)} %collective-permute-done.5.cr_ref) | copy-start | bytes 98308
  96.2 0.9 copy-start.4
  104.8 0.9 copy-start.1
  105.7 20.5 %copy-start.15 = (bf16[1056,128]{1,0:T(8,128)(2,1)S(1)}, bf16[1056,128]{1,0:T(8,128)(2,1)}, u32[]{:S(2)}) copy-start(bf16[1056,128]{1,0:T(8,128)(2,1)} %get-tuple-element.29) | copy-start | bytes 811012
  105.7 21.9 %copy-start.14 = (bf16[1056,128]{1,0:T(8,128)(2,1)S(1)}, bf16[1056,128]{1,0:T(8,128)(2,1)}, u32[]{:S(2)}) copy-start(bf16[1056,128]{1,0:T(8,128)(2,1)} %get-tuple-element.31) | copy-start | bytes 811012
  119.6 37.0 %all-to-all-start.1 = ((bf16[128,16,128]{2,1,0:T(8,128)(2,1)}), bf16[128,16,128]{2,1,0:T(8,128)(2,1)S(1)}, u32[]{:S(2)}, u32[]{:S(2)}) async-start(bf16[128,16,128]{2,1,0:T(8,128)(2,1)} %bitcast.42), calls=%async_computation.1 | async-start | bytes 1048576 | tf_op jit(solution)/shard_map/all_to_all | solution.py:583
  126.1 19.8 %copy-start.13 = (bf16[128,128]{1,0:T(8,128)(2,1)}, bf16[128,128]{1,0:T(8,128)(2,1)S(1)}, u32[]{:S(2)}) copy-start(bf16[128,128]{1,0:T(8,128)(2,1)S(1)} %collective-permute-done.4.cl_ref) | copy-start | bytes 98308
  126.2 18.1 %collective-permute-start.6 = (bf16[1056,128]{1,0:T(8,128)(2,1)S(1)}, bf16[1056,128]{1,0:T(8,128)(2,1)S(1)}, u32[]{:S(2)}, u32[]{:S(2)}) collective-permute-start(bf16[1056,128]{1,0:T(8,128)(2,1)S(1)} %maximum_dynamic-update-slice_fusion.2), channel_id=1, source_target_pairs={{0,4},{4,8},{8,12},{12,16},{16,20},{20,24},{24,28},{28,32},{32,36}... | collective-permute-start | bytes 811016 | tf_op jit(solution)/shard_map/ppermute | solution.py:512
  127.6 18.3 %collective-permute-start.7 = (bf16[1056,128]{1,0:T(8,128)(2,1)S(1)}, bf16[1056,128]{1,0:T(8,128)(2,1)S(1)}, u32[]{:S(2)}, u32[]{:S(2)}) collective-permute-start(bf16[1056,128]{1,0:T(8,128)(2,1)S(1)} %maximum_dynamic-update-slice_fusion.3), channel_id=1, source_target_pairs={{0,124},{4,0},{8,4},{12,8},{16,12},{20,16},{24,20},{28,24},{32,28}... | collective-permute-start | bytes 811016 | tf_op jit(solution)/shard_map/ppermute | solution.py:512
  144.3 1.6 %copy-start.9 = (bf16[1056,128]{1,0:T(8,128)(2,1)}, bf16[1056,128]{1,0:T(8,128)(2,1)S(1)}, u32[]{:S(2)}) copy-start(bf16[1056,128]{1,0:T(8,128)(2,1)S(1)} %collective-permute-done.6.top_ref) | copy-start | bytes 811012
  145.9 0.7 copy-start.11
  156.6 0.8 copy-start.2

commit v2 on v1

--- a/solution.py
+++ b/solution.py
@@ -89,9 +89,7 @@
     )(x)
 
 
-def cprep_body(x_ref, cols_ref, o_ref, east_ref, west_ref):
-    east_ref[0:128, :] = cols_ref[...]
-    west_ref[0:128, :] = cols_ref[...]
+def cprep_body(x_ref, o_ref, east_ref, west_ref):
     r, k = iota((256, 256), 0), iota((256, 256), 1)
     perm = onehot((r % 16) * 16 + r // 16 == k)
     for g in range(4):
@@ -103,26 +101,26 @@
             for y in range(16):
                 v = out[y * 16 : y * 16 + 16, z * 128 : z * 128 + 128]
                 o_ref[z, y, g * 16 : g * 16 + 16, :] = v
-                row = 128 + z * 128 + (y % 2) * 64 + g * 16
+                row = z * 128 + (y % 2) * 64 + g * 16
                 if y >= 14:
                     east_ref[row : row + 16, :] = v
                 if y < 2:
                     west_ref[row : row + 16, :] = v
 
 
-def cprep(x, cols):
+def cprep(x):
     return pl.pallas_call(
         cprep_body,
-        in_specs=vm(2),
+        in_specs=vm(1),
         out_specs=vm(3),
         out_shape=[
             jax.ShapeDtypeStruct((2, 16, 64, 128), BF),
-            jax.ShapeDtypeStruct((384, 128), BF),
-            jax.ShapeDtypeStruct((384, 128), BF),
+            jax.ShapeDtypeStruct((256, 128), BF),
+            jax.ShapeDtypeStruct((256, 128), BF),
         ],
         interpret=INTERPRET,
         name="cprep",
-    )(x, cols)
+    )(x)
 
 
 def weights_body(f1_ref, f2_ref, c1_ref, c2_ref, wf1_ref, wf2_ref, wa_ref, wb_ref, wc_ref, w0_ref):
@@ -548,21 +546,23 @@
     n = lax.axis_index("narrow")
     reaches = jnp.where(w % 2 == 1, w < 31, w > 0).astype(jnp.int32)
     at = jnp.stack([w // 8, w % 8, n, w, w % 2, reaches])
-    rows, down, up, cols = prep(fine_in)
-    ct, east, west = cprep(coarse_in, cols)
-    from_left = shift(east, "narrow", 1)
-    from_right = shift(west, "narrow", -1)
-    top, bottom = across_y(down, up, from_left, from_right)
-    wf1, wf2, wa, wb, wc = weights(taps(w_fine1), taps(w_fine2), taps(w_coarse1), taps(w_coarse2))
+    ct, east, west = cprep(coarse_in)
+    before = shift(east, "narrow", 1)
+    after = shift(west, "narrow", -1)
     slab = jnp.concatenate(
         [
-            jnp.where(n > 0, from_left[128:], jnp.zeros((), BF)).reshape(2, 2, 64, 128),
+            kept(n > 0, before).reshape(2, 2, 64, 128),
             ct,
-            jnp.where(n < 3, from_right[128:], jnp.zeros((), BF)).reshape(2, 2, 64, 128),
+            kept(n < 3, after).reshape(2, 2, 64, 128),
         ],
         axis=1,
     )
     mate = lax.ppermute(slab, "wide", [(i, i ^ 1) for i in range(32)])
+    rows, down, up, cols = prep(fine_in)
+    from_left = shift(cols, "narrow", 1)
+    from_right = shift(cols, "narrow", -1)
+    top, bottom = across_y(down, up, from_left, from_right)
+    wf1, wf2, wa, wb, wc = weights(taps(w_fine1), taps(w_fine2), taps(w_coarse1), taps(w_coarse2))
     hops = [(i, i + 2 - 4 * (i % 2)) for i in range(32)]
     far = lax.ppermute(mate, "wide", [(i, j % 32) for i, j in hops])
     hidden, pooled, hcols, hdown, hup = fine1(

time: 163 us -> 166 us (1.018)
  starting transfers between devices: 46.8 us -> 52.4 us
  waiting for transfers between devices: 41.1 us -> 38 us
    ppermute x1, starting transfers between devices: 7.04 us -> 3.32 us  [local(): ends = lax.ppermute(pooled, ('wide', 'narrow'), turns(1))]
    ppermute x8 -> x10, starting transfers between devices: 20.9 us -> 24.1 us  [shift(): lax.ppermute(array, axis, [(i, (i + by) % count) for i in range(count)])]
    ppermute x1, starting transfers between devices: 0.01 us -> 3.12 us  [local(): far = lax.ppermute(mate, 'wide', [(i, j % 32) for i, j in hops])]
    ppermute x1, waiting for transfers between devices: 3.84 us -> 2.01 us  [local(): turned = lax.ppermute(pooled, ('wide', 'narrow'), turns(0))]
    ppermute x1, waiting for transfers between devices: 7.48 us -> 5.71 us  [local(): far = lax.ppermute(mate, 'wide', [(i, j % 32) for i, j in hops])]
    ppermute x8 -> x10, waiting for transfers between devices: 22.7 us -> 23.7 us  [shift(): lax.ppermute(array, axis, [(i, (i + by) % count) for i in range(count)])]
  transfers between devices with their start and end apart: 14 -> 16, of which waited for: 9 -> 9; matrix products, arithmetic and copies ran while one was open for 2% -> 2% of each run, Pallas kernels for 26% -> 27%
where the time goes in v2:
time: 166 us; the launch traced here: 165 us
  Pallas kernels  66.6 us (40%)
  starting transfers between devices  52.4 us (32%)
  waiting for transfers between devices  38 us (23%)
  local copies, waits for them, and re-layouts  5.77 us (3%)
    ppermute x10, starting transfers between devices, shift(): lax.ppermute(array, axis, [(i, (i + by) % count) for i in range(count)])  24.1 us
    ppermute x10, waiting for transfers between devices, shift(): lax.ppermute(array, axis, [(i, (i + by) % count) for i in range(count)])  23.7 us
    pallas_call x2, Pallas kernels, conv1a(): pl.pallas_call(functools.partial(conv1a_body, name == 'distant'), in_spec...  15.4 us
    pallas_call x1, Pallas kernels, coarse(): pl.pallas_call(coarse_body, grid_spec=pltpu.PrefetchScalarGridSpec(num_sc...  13.9 us
    all_to_all x1, starting transfers between devices, local(): got = lax.all_to_all(parcels.reshape(32, 96, 128), 'wide', 0, 0, tiled=True)  11 us
    pallas_call x1, Pallas kernels, fine1(): pl.pallas_call(fine1_body, in_specs=[pl.BlockSpec(memory_space=pltpu.SMEM...  10.6 us
    pallas_call x1, Pallas kernels, fine2(): pl.pallas_call(fine2_body, in_specs=[pl.BlockSpec(memory_space=pltpu.SMEM...  9.98 us
    all_to_all x1, starting transfers between devices, local(): lax.all_to_all(context.reshape(128, 16, 128), ('wide', 'narrow'), 0, 0, t...  7.99 us
  transfers between devices with their start and end apart: 16, of which 9 were waited for; matrix products, arithmetic and copies ran while one was open for 2% of the time, Pallas kernels for 27%

profile of v2, /device:TPU:1, one launch (start us, length us, event | category | flops | bytes accessed | tf_op | source)
XLA Modules:
  0.0 165.1 jit_solution(3665225889886674362)
XLA Ops:
  0.6 6.3 %prep.1 = (bf16[64,128,128]{2,1,0:T(8,128)(2,1)}, bf16[1056,128]{1,0:T(8,128)(2,1)}, bf16[1056,128]{1,0:T(8,128)(2,1)}, bf16[128,128]{1,0:T(8,128)(2,1)}) custom-call(bf16[16,64,8,128]{3,2,1,0:T(8,128)(2,1)} %x_ref.2), custom_call_target="tpu_custom_call" | custom-call | tf_op jit(solution)/shard_map/prep/pallas_call | solution.py:70
  6.9 1.5 collective-permute-start.1
  8.3 3.0 %collective-permute-start = (bf16[128,128]{1,0:T(8,128)(2,1)}, bf16[128,128]{1,0:T(8,128)(2,1)S(1)}, u32[]{:S(2)}, u32[]{:S(2)}) collective-permute-start(bf16[128,128]{1,0:T(8,128)(2,1)} %get-tuple-element.23), channel_id=1, source_target_pairs={{0,1},{1,2},{2,3},{3,0},{4,5},{5,6},{6,7},{7,4},{8,9},{9,10},{10,1... | collective-permute-start | bytes 98312 | tf_op jit(solution)/shard_map/ppermute | solution.py:510
  11.3 2.2 %cprep.1 = (bf16[2,16,64,128]{3,2,1,0:T(8,128)(2,1)}, bf16[256,128]{1,0:T(8,128)(2,1)}, bf16[256,128]{1,0:T(8,128)(2,1)}) custom-call(bf16[64,2,16,128]{3,2,1,0:T(8,128)(2,1)} %x_ref.3), custom_call_target="tpu_custom_call" | custom-call | tf_op jit(solution)/shard_map/cprep/pallas_call | solution.py:112
  13.5 3.2 %collective-permute-start.10 = (bf16[256,128]{1,0:T(8,128)(2,1)}, bf16[256,128]{1,0:T(8,128)(2,1)S(1)}, u32[]{:S(2)}, u32[]{:S(2)}) collective-permute-start(bf16[256,128]{1,0:T(8,128)(2,1)} %get-tuple-element.32), channel_id=1, source_target_pairs={{0,1},{1,2},{2,3},{3,0},{4,5},{5,6},{6,7},{7,4},{8,9},{9,10},{10,1... | collective-permute-start | bytes 196616 | tf_op jit(solution)/shard_map/ppermute | solution.py:510
  16.8 3.2 %weights.1 = (bf16[128,1536]{1,0:T(8,128)(2,1)}, bf16[128,1536]{1,0:T(8,128)(2,1)}, bf16[64,1728]{1,0:T(8,128)(2,1)}, bf16[64,432]{1,0:T(8,128)(2,1)}, bf16[64,1728]{1,0:T(8,128)(2,1)}) custom-call(bf16[27,16,16]{2,1,0:T(8,128)(2,1)} %bitcast.51, bf16[27,16,16]{2,1,0:T(8,128)(2,1)} %bitcast.52, bf16[27,64,80]{2,1,0:T(8,128)(2,1)} %bitcast.47, ...), custom_call_target="tpu_custom_call" | custom-call | tf_op jit(solution)/shard_map/weights/pallas_call | solution.py:146
  21.2 1.0 collective-permute-start.2
  22.8 5.7 %collective-permute-start.3 = (bf16[1056,128]{1,0:T(8,128)(2,1)}, bf16[1056,128]{1,0:T(8,128)(2,1)S(1)}, u32[]{:S(2)}, u32[]{:S(2)}) collective-permute-start(bf16[1056,128]{1,0:T(8,128)(2,1)} %maximum_dynamic-update-slice_fusion.1), channel_id=1, source_target_pairs={{0,124},{4,0},{8,4},{12,8},{16,12},{20,16},{24,20},{28,24},{32,28}... | collective-permute-start | bytes 811016 | tf_op jit(solution)/shard_map/ppermute | solution.py:510
  28.5 5.7 %collective-permute-done.2.top_ref = bf16[1056,128]{1,0:T(8,128)(2,1)S(1)} collective-permute-done((bf16[1056,128]{1,0:T(8,128)(2,1)}, bf16[1056,128]{1,0:T(8,128)(2,1)S(1)}, u32[]{:S(2)}, u32[]{:S(2)}) %collective-permute-start.2) | collective-permute-done | bytes 270368 | tf_op jit(solution)/shard_map/ppermute | solution.py:510
  34.3 2.6 %collective-permute-done.3.bot_ref = bf16[1056,128]{1,0:T(8,128)(2,1)S(1)} collective-permute-done((bf16[1056,128]{1,0:T(8,128)(2,1)}, bf16[1056,128]{1,0:T(8,128)(2,1)S(1)}, u32[]{:S(2)}, u32[]{:S(2)}) %collective-permute-start.3) | collective-permute-done | bytes 270368 | tf_op jit(solution)/shard_map/ppermute | solution.py:510
  37.6 10.6 %fine1.1 = (bf16[64,128,128]{2,1,0:T(8,128)(2,1)}, bf16[512,128]{1,0:T(8,128)(2,1)}, bf16[128,128]{1,0:T(8,128)(2,1)}, bf16[1056,128]{1,0:T(8,128)(2,1)}, bf16[1056,128]{1,0:T(8,128)(2,1)}) custom-call(s32[6]{0:T(128)} %stack.56.at_ref, bf16[64,128,128]{2,1,0:T(8,128)(2,1)} %get-tuple-element.21.x_ref, bf16[1056,128]{1,0:T(8,128)(2,1)} %copy-done.8, ...), custom_call_target="tpu_custom_call" | custom-call | tf_op jit(solution)/shard_map/fine1/pallas_call | solution.py:271
  48.1 3.3 %collective-permute-start.9 = (bf16[512,128]{1,0:T(8,128)(2,1)}, bf16[512,128]{1,0:T(8,128)(2,1)S(1)}, u32[]{:S(2)}, u32[]{:S(2)}) collective-permute-start(bf16[512,128]{1,0:T(8,128)(2,1)} %get-tuple-element.31), channel_id=1, source_target_pairs={{0,3},{1,35},{2,67},{3,99},{4,4},{5,36},{6,68},{7,100},{8,8},{9,40... | collective-permute-start | bytes 393224 | tf_op jit(solution)/shard_map/ppermute | solution.py:572
  51.5 2.8 %collective-permute-start.8 = (bf16[512,128]{1,0:T(8,128)(2,1)}, bf16[512,128]{1,0:T(8,128)(2,1)S(1)}, u32[]{:S(2)}, u32[]{:S(2)}) collective-permute-start(bf16[512,128]{1,0:T(8,128)(2,1)} %get-tuple-element.31), channel_id=1, source_target_pairs={{0,0},{1,32},{2,64},{3,96},{4,4},{5,36},{6,68},{7,100},{8,8},{9,40... | collective-permute-start | bytes 393224 | tf_op jit(solution)/shard_map/ppermute | solution.py:571
  54.4 1.8 %collective-permute-done.9 = bf16[512,128]{1,0:T(8,128)(2,1)S(1)} collective-permute-done((bf16[512,128]{1,0:T(8,128)(2,1)}, bf16[512,128]{1,0:T(8,128)(2,1)S(1)}, u32[]{:S(2)}, u32[]{:S(2)}) %collective-permute-start.9) | collective-permute-done | bytes 131104 | tf_op jit(solution)/shard_map/ppermute | solution.py:572
  56.3 2.0 %collective-permute-done.8 = bf16[512,128]{1,0:T(8,128)(2,1)S(1)} collective-permute-done((bf16[512,128]{1,0:T(8,128)(2,1)}, bf16[512,128]{1,0:T(8,128)(2,1)S(1)}, u32[]{:S(2)}, u32[]{:S(2)}) %collective-permute-start.8) | collective-permute-done | bytes 131104 | tf_op jit(solution)/shard_map/ppermute | solution.py:571
  58.5 1.0 copy.14
  59.5 11.0 %all-to-all-start = ((bf16[32,96,128]{2,1,0:T(8,128)(2,1)}), bf16[32,96,128]{2,1,0:T(8,128)(2,1)S(1)}, u32[]{:S(2)}, u32[]{:S(2)}) async-start(bf16[32,96,128]{2,1,0:T(8,128)(2,1)} %bitcast.24), calls=%async_computation | async-start | bytes 1572864 | tf_op jit(solution)/shard_map/all_to_all | solution.py:576
  70.5 4.8 %collective-permute-done.12.second_ref = bf16[2,20,64,128]{3,2,1,0:T(8,128)(2,1)S(1)} collective-permute-done((bf16[2,20,64,128]{3,2,1,0:T(8,128)(2,1)S(1)}, bf16[2,20,64,128]{3,2,1,0:T(8,128)(2,1)S(1)}, u32[]{:S(2)}, u32[]{:S(2)}) %collective-permute-start.12) | collective-permute-done | bytes 655392 | tf_op jit(solution)/shard_map/ppermute | solution.py:560
  75.3 3.1 %collective-permute-start.13 = (bf16[2,20,64,128]{3,2,1,0:T(8,128)(2,1)S(1)}, bf16[2,20,64,128]{3,2,1,0:T(8,128)(2,1)S(1)}, u32[]{:S(2)}, u32[]{:S(2)}) collective-permute-start(bf16[2,20,64,128]{3,2,1,0:T(8,128)(2,1)S(1)} %collective-permute-done.12.second_ref), channel_id=1, source_target_pairs={{0,8},{4,124},{8,16},{12,4},{16,24},{20,12},{24,32},{28,20},{32,40... | collective-permute-start | bytes 1966088 | tf_op jit(solution)/shard_map/ppermute | solution.py:567
  78.4 3.2 %collective-permute-start.4 = (bf16[128,128]{1,0:T(8,128)(2,1)S(1)}, bf16[128,128]{1,0:T(8,128)(2,1)S(1)}, u32[]{:S(2)}, u32[]{:S(2)}) collective-permute-start(bf16[128,128]{1,0:T(8,128)(2,1)S(1)} %copy-done.16), channel_id=1, source_target_pairs={{0,1},{1,2},{2,3},{3,0},{4,5},{5,6},{6,7},{7,4},{8,9},{9,10},{10,1... | collective-permute-start | bytes 98312 | tf_op jit(solution)/shard_map/ppermute | solution.py:510
  81.7 2.2 %collective-permute-done.5.cr_ref = bf16[128,128]{1,0:T(8,128)(2,1)S(1)} collective-permute-done((bf16[128,128]{1,0:T(8,128)(2,1)S(1)}, bf16[128,128]{1,0:T(8,128)(2,1)S(1)}, u32[]{:S(2)}, u32[]{:S(2)}) %collective-permute-start.5) | collective-permute-done | bytes 32800 | tf_op jit(solution)/shard_map/ppermute | solution.py:510
  83.8 7.7 %shard_map.122.near_ref = f32[18,64,256]{2,1,0:T(8,128)} custom-call(s32[6]{0:T(128)} %stack.56.at_ref, bf16[2,20,64,128]{3,2,1,0:T(8,128)(2,1)} %copy-done, bf16[2,20,64,128]{3,2,1,0:T(8,128)(2,1)} %copy-done.3, bf16[64,1728]{1,0:T(8,128)(2,1)} %get-tuple-element.35.w_ref, f32[1,64]{1,0:T(1,128)} %bitcast.53), custom_call_target="tpu_custom_call" | custom-call | tf_op jit(solution)/shard_map/pallas_call | solution.py:394
  91.5 5.7 %collective-permute-done.13.first_ref = bf16[2,20,64,128]{3,2,1,0:T(8,128)(2,1)S(1)} collective-permute-done((bf16[2,20,64,128]{3,2,1,0:T(8,128)(2,1)S(1)}, bf16[2,20,64,128]{3,2,1,0:T(8,128)(2,1)S(1)}, u32[]{:S(2)}, u32[]{:S(2)}) %collective-permute-start.13) | collective-permute-done | bytes 655392 | tf_op jit(solution)/shard_map/ppermute | solution.py:567
  98.1 7.7 %shard_map.123.far_ref = f32[18,64,256]{2,1,0:T(8,128)} custom-call(s32[6]{0:T(128)} %stack.56.at_ref, bf16[2,20,64,128]{3,2,1,0:T(8,128)(2,1)} %copy-done.4, bf16[2,20,64,128]{3,2,1,0:T(8,128)(2,1)} %copy-done, bf16[64,1728]{1,0:T(8,128)(2,1)} %get-tuple-element.35.w_ref, f32[1,64]{1,0:T(1,128)} %bitcast.54), custom_call_target="tpu_custom_call" | custom-call | tf_op jit(solution)/shard_map/pallas_call | solution.py:394
  106.7 13.9 %coarse.1 = (bf16[64,2,16,128]{3,2,1,0:T(8,128)(2,1)}, bf16[4,8,4,16,128]{4,3,2,1,0:T(8,128)(2,1)}) custom-call(s32[6]{0:T(128)} %stack.56.at_ref, bf16[32,2,48,128]{3,2,1,0:T(8,128)(2,1)} %bitcast.40, f32[18,64,256]{2,1,0:T(8,128)} %shard_map.122.near_ref, f32[18,64,256]{2,1,0:T(8,128)} %shard_map.123.far_ref, bf16[64,432]{1,0:T(8,128)(2,1)} %get-tuple-element.36.w1_ref, ...), custom_call_target="tpu_custom_call" | custom-call | tf_op jit(solution)/shard_map/coarse/pallas_call | solution.py:477
  120.6 8.0 %all-to-all-start.1 = ((bf16[128,16,128]{2,1,0:T(8,128)(2,1)}), bf16[128,16,128]{2,1,0:T(8,128)(2,1)S(1)}, u32[]{:S(2)}, u32[]{:S(2)}) async-start(bf16[128,16,128]{2,1,0:T(8,128)(2,1)} %bitcast.42), calls=%async_computation.1 | async-start | bytes 1048576 | tf_op jit(solution)/shard_map/all_to_all | solution.py:583
  128.6 1.4 collective-permute-start.6
  130.1 5.1 %collective-permute-start.7 = (bf16[1056,128]{1,0:T(8,128)(2,1)S(1)}, bf16[1056,128]{1,0:T(8,128)(2,1)S(1)}, u32[]{:S(2)}, u32[]{:S(2)}) collective-permute-start(bf16[1056,128]{1,0:T(8,128)(2,1)S(1)} %maximum_dynamic-update-slice_fusion.3), channel_id=1, source_target_pairs={{0,124},{4,0},{8,4},{12,8},{16,12},{20,16},{24,20},{28,24},{32,28}... | collective-permute-start | bytes 811016 | tf_op jit(solution)/shard_map/ppermute | solution.py:510
  135.2 11.6 %collective-permute-done.6.top_ref = bf16[1056,128]{1,0:T(8,128)(2,1)S(1)} collective-permute-done((bf16[1056,128]{1,0:T(8,128)(2,1)S(1)}, bf16[1056,128]{1,0:T(8,128)(2,1)S(1)}, u32[]{:S(2)}, u32[]{:S(2)}) %collective-permute-start.6) | collective-permute-done | bytes 270368 | tf_op jit(solution)/shard_map/ppermute | solution.py:510
  146.7 1.6 collective-permute-done.7.bot_ref
  149.1 10.0 %fine2.1.t_ref = bf16[64,128,128]{2,1,0:T(8,128)(2,1)} custom-call(s32[6]{0:T(128)} %stack.56.at_ref, bf16[64,128,128]{2,1,0:T(8,128)(2,1)} %get-tuple-element.26.x_ref, bf16[1056,128]{1,0:T(8,128)(2,1)} %copy-done.6, bf16[1056,128]{1,0:T(8,128)(2,1)} %copy-done.7, bf16[128,128]{1,0:T(8,128)(2,1)} %copy-done.13, bf16[128,128]{1,0:T(8,128)(2,1)} %copy-done.12, ...), custom_call_target="tpu_custom_call" | custom-call | tf_op jit(solution)/shard_map/fine2/pallas_call | solution.py:301
  159.9 5.2 %final.1 = bf16[16,64,8,128]{3,2,1,0:T(8,128)(2,1)} custom-call(s32[6]{0:T(128)} %stack.56.at_ref, bf16[64,128,128]{2,1,0:T(8,128)(2,1)} %fine2.1.t_ref, bf16[32,4,16,128]{3,2,1,0:T(8,128)(2,1)} %bitcast.41), custom_call_target="tpu_custom_call" | custom-call | tf_op jit(solution)/shard_map/final/pallas_call | solution.py:332
  (59 shorter events, 6.3 us)
Async XLA Ops:
  6.9 13.7 %collective-permute-start.1 = (bf16[128,128]{1,0:T(8,128)(2,1)}, bf16[128,128]{1,0:T(8,128)(2,1)S(1)}, u32[]{:S(2)}, u32[]{:S(2)}) collective-permute-start(bf16[128,128]{1,0:T(8,128)(2,1)} %get-tuple-element.23), channel_id=1, source_target_pairs={{0,3},{1,0},{2,1},{3,2},{4,7},{5,4},{6,5},{7,6},{8,11},{9,8},{10,9... | collective-permute-start | bytes 98312 | tf_op jit(solution)/shard_map/ppermute | solution.py:510
  8.3 12.2 %collective-permute-start = (bf16[128,128]{1,0:T(8,128)(2,1)}, bf16[128,128]{1,0:T(8,128)(2,1)S(1)}, u32[]{:S(2)}, u32[]{:S(2)}) collective-permute-start(bf16[128,128]{1,0:T(8,128)(2,1)} %get-tuple-element.23), channel_id=1, source_target_pairs={{0,1},{1,2},{2,3},{3,0},{4,5},{5,6},{6,7},{7,4},{8,9},{9,10},{10,1... | collective-permute-start | bytes 98312 | tf_op jit(solution)/shard_map/ppermute | solution.py:510
  13.5 15.0 %collective-permute-start.11 = (bf16[256,128]{1,0:T(8,128)(2,1)}, bf16[256,128]{1,0:T(8,128)(2,1)S(1)}, u32[]{:S(2)}, u32[]{:S(2)}) collective-permute-start(bf16[256,128]{1,0:T(8,128)(2,1)} %get-tuple-element.34), channel_id=1, source_target_pairs={{0,3},{1,0},{2,1},{3,2},{4,7},{5,4},{6,5},{7,6},{8,11},{9,8},{10,9... | collective-permute-start | bytes 196616 | tf_op jit(solution)/shard_map/ppermute | solution.py:510
  13.5 15.0 %collective-permute-start.10 = (bf16[256,128]{1,0:T(8,128)(2,1)}, bf16[256,128]{1,0:T(8,128)(2,1)S(1)}, u32[]{:S(2)}, u32[]{:S(2)}) collective-permute-start(bf16[256,128]{1,0:T(8,128)(2,1)} %get-tuple-element.32), channel_id=1, source_target_pairs={{0,1},{1,2},{2,3},{3,0},{4,5},{5,6},{6,7},{7,4},{8,9},{9,10},{10,1... | collective-permute-start | bytes 196616 | tf_op jit(solution)/shard_map/ppermute | solution.py:510
  16.8 37.5 %copy-start.5 = (bf16[2,16,64,128]{3,2,1,0:T(8,128)(2,1)S(1)}, bf16[2,16,64,128]{3,2,1,0:T(8,128)(2,1)}, u32[]{:S(2)}) copy-start(bf16[2,16,64,128]{3,2,1,0:T(8,128)(2,1)} %get-tuple-element.33) | copy-start | bytes 1572868
  20.6 16.3 %copy-start.10 = (bf16[128,128]{1,0:T(8,128)(2,1)}, bf16[128,128]{1,0:T(8,128)(2,1)S(1)}, u32[]{:S(2)}) copy-start(bf16[128,128]{1,0:T(8,128)(2,1)S(1)} %collective-permute-done.1.cr_ref) | copy-start | bytes 98308
  20.6 16.3 %copy-start.11 = (bf16[128,128]{1,0:T(8,128)(2,1)}, bf16[128,128]{1,0:T(8,128)(2,1)S(1)}, u32[]{:S(2)}) copy-start(bf16[128,128]{1,0:T(8,128)(2,1)S(1)} %collective-permute-done.cl_ref) | copy-start | bytes 98308
  21.2 13.1 %collective-permute-start.2 = (bf16[1056,128]{1,0:T(8,128)(2,1)}, bf16[1056,128]{1,0:T(8,128)(2,1)S(1)}, u32[]{:S(2)}, u32[]{:S(2)}) collective-permute-start(bf16[1056,128]{1,0:T(8,128)(2,1)} %maximum_dynamic-update-slice_fusion), channel_id=1, source_target_pairs={{0,4},{4,8},{8,12},{12,16},{16,20},{20,24},{24,28},{28,32},{32,36}... | collective-permute-start | bytes 811016 | tf_op jit(solution)/shard_map/ppermute | solution.py:510
  22.8 14.1 %collective-permute-start.3 = (bf16[1056,128]{1,0:T(8,128)(2,1)}, bf16[1056,128]{1,0:T(8,128)(2,1)S(1)}, u32[]{:S(2)}, u32[]{:S(2)}) collective-permute-start(bf16[1056,128]{1,0:T(8,128)(2,1)} %maximum_dynamic-update-slice_fusion.1), channel_id=1, source_target_pairs={{0,124},{4,0},{8,4},{12,8},{16,12},{20,16},{24,20},{28,24},{32,28}... | collective-permute-start | bytes 811016 | tf_op jit(solution)/shard_map/ppermute | solution.py:510
  34.3 2.6 %copy-start.8 = (bf16[1056,128]{1,0:T(8,128)(2,1)}, bf16[1056,128]{1,0:T(8,128)(2,1)S(1)}, u32[]{:S(2)}) copy-start(bf16[1056,128]{1,0:T(8,128)(2,1)S(1)} %collective-permute-done.2.top_ref) | copy-start | bytes 811012
  48.1 8.1 %collective-permute-start.9 = (bf16[512,128]{1,0:T(8,128)(2,1)}, bf16[512,128]{1,0:T(8,128)(2,1)S(1)}, u32[]{:S(2)}, u32[]{:S(2)}) collective-permute-start(bf16[512,128]{1,0:T(8,128)(2,1)} %get-tuple-element.31), channel_id=1, source_target_pairs={{0,3},{1,35},{2,67},{3,99},{4,4},{5,36},{6,68},{7,100},{8,8},{9,40... | collective-permute-start | bytes 393224 | tf_op jit(solution)/shard_map/ppermute | solution.py:572
  51.5 6.8 %collective-permute-start.8 = (bf16[512,128]{1,0:T(8,128)(2,1)}, bf16[512,128]{1,0:T(8,128)(2,1)S(1)}, u32[]{:S(2)}, u32[]{:S(2)}) collective-permute-start(bf16[512,128]{1,0:T(8,128)(2,1)} %get-tuple-element.31), channel_id=1, source_target_pairs={{0,0},{1,32},{2,64},{3,96},{4,4},{5,36},{6,68},{7,100},{8,8},{9,40... | collective-permute-start | bytes 393224 | tf_op jit(solution)/shard_map/ppermute | solution.py:571
  54.3 5.2 %copy-start = (bf16[2,20,64,128]{3,2,1,0:T(8,128)(2,1)}, bf16[2,20,64,128]{3,2,1,0:T(8,128)(2,1)S(1)}, u32[]{:S(2)}) copy-start(bf16[2,20,64,128]{3,2,1,0:T(8,128)(2,1)S(1)} %pad_maximum_fusion.first_ref.second_ref) | copy-start | bytes 1966084
  54.4 20.9 %collective-permute-start.12 = (bf16[2,20,64,128]{3,2,1,0:T(8,128)(2,1)S(1)}, bf16[2,20,64,128]{3,2,1,0:T(8,128)(2,1)S(1)}, u32[]{:S(2)}, u32[]{:S(2)}) collective-permute-start(bf16[2,20,64,128]{3,2,1,0:T(8,128)(2,1)S(1)} %pad_maximum_fusion.first_ref.second_ref), channel_id=1, source_target_pairs={{0,4},{4,0},{8,12},{12,8},{16,20},{20,16},{24,28},{28,24},{32,36},... | collective-permute-start | bytes 1966088 | tf_op jit(solution)/shard_map/ppermute | solution.py:560
  58.4 20.0 %copy-start.16 = (bf16[128,128]{1,0:T(8,128)(2,1)S(1)}, bf16[128,128]{1,0:T(8,128)(2,1)}, u32[]{:S(2)}) copy-start(bf16[128,128]{1,0:T(8,128)(2,1)} %get-tuple-element.28) | copy-start | bytes 98308
  59.5 46.3 %all-to-all-start = ((bf16[32,96,128]{2,1,0:T(8,128)(2,1)}), bf16[32,96,128]{2,1,0:T(8,128)(2,1)S(1)}, u32[]{:S(2)}, u32[]{:S(2)}) async-start(bf16[32,96,128]{2,1,0:T(8,128)(2,1)} %bitcast.24), calls=%async_computation | async-start | bytes 1572864 | tf_op jit(solution)/shard_map/all_to_all | solution.py:576
  75.3 8.6 %copy-start.3 = (bf16[2,20,64,128]{3,2,1,0:T(8,128)(2,1)}, bf16[2,20,64,128]{3,2,1,0:T(8,128)(2,1)S(1)}, u32[]{:S(2)}) copy-start(bf16[2,20,64,128]{3,2,1,0:T(8,128)(2,1)S(1)} %collective-permute-done.12.second_ref) | copy-start | bytes 1966084
  75.3 22.0 %collective-permute-start.13 = (bf16[2,20,64,128]{3,2,1,0:T(8,128)(2,1)S(1)}, bf16[2,20,64,128]{3,2,1,0:T(8,128)(2,1)S(1)}, u32[]{:S(2)}, u32[]{:S(2)}) collective-permute-start(bf16[2,20,64,128]{3,2,1,0:T(8,128)(2,1)S(1)} %collective-permute-done.12.second_ref), channel_id=1, source_target_pairs={{0,8},{4,124},{8,16},{12,4},{16,24},{20,12},{24,32},{28,20},{32,40... | collective-permute-start | bytes 1966088 | tf_op jit(solution)/shard_map/ppermute | solution.py:567
  78.4 5.4 %collective-permute-start.5 = (bf16[128,128]{1,0:T(8,128)(2,1)S(1)}, bf16[128,128]{1,0:T(8,128)(2,1)S(1)}, u32[]{:S(2)}, u32[]{:S(2)}) collective-permute-start(bf16[128,128]{1,0:T(8,128)(2,1)S(1)} %copy-done.16), channel_id=1, source_target_pairs={{0,3},{1,0},{2,1},{3,2},{4,7},{5,4},{6,5},{7,6},{8,11},{9,8},{10,9... | collective-permute-start | bytes 98312 | tf_op jit(solution)/shard_map/ppermute | solution.py:510
  78.4 50.2 %collective-permute-start.4 = (bf16[128,128]{1,0:T(8,128)(2,1)S(1)}, bf16[128,128]{1,0:T(8,128)(2,1)S(1)}, u32[]{:S(2)}, u32[]{:S(2)}) collective-permute-start(bf16[128,128]{1,0:T(8,128)(2,1)S(1)} %copy-done.16), channel_id=1, source_target_pairs={{0,1},{1,2},{2,3},{3,0},{4,5},{5,6},{6,7},{7,4},{8,9},{9,10},{10,1... | collective-permute-start | bytes 98312 | tf_op jit(solution)/shard_map/ppermute | solution.py:510
  83.8 22.0 %copy-start.12 = (bf16[128,128]{1,0:T(8,128)(2,1)}, bf16[128,128]{1,0:T(8,128)(2,1)S(1)}, u32[]{:S(2)}) copy-start(bf16[128,128]{1,0:T(8,128)(2,1)S(1)} %collective-permute-done.5.cr_ref) | copy-start | bytes 98308
  97.2 0.9 copy-start.4
  105.8 0.9 copy-start.1
  106.7 21.9 %copy-start.15 = (bf16[1056,128]{1,0:T(8,128)(2,1)S(1)}, bf16[1056,128]{1,0:T(8,128)(2,1)}, u32[]{:S(2)}) copy-start(bf16[1056,128]{1,0:T(8,128)(2,1)} %get-tuple-element.27) | copy-start | bytes 811012
  106.7 23.4 %copy-start.14 = (bf16[1056,128]{1,0:T(8,128)(2,1)S(1)}, bf16[1056,128]{1,0:T(8,128)(2,1)}, u32[]{:S(2)}) copy-start(bf16[1056,128]{1,0:T(8,128)(2,1)} %get-tuple-element.29) | copy-start | bytes 811012
  120.6 38.5 %all-to-all-start.1 = ((bf16[128,16,128]{2,1,0:T(8,128)(2,1)}), bf16[128,16,128]{2,1,0:T(8,128)(2,1)S(1)}, u32[]{:S(2)}, u32[]{:S(2)}) async-start(bf16[128,16,128]{2,1,0:T(8,128)(2,1)} %bitcast.42), calls=%async_computation.1 | async-start | bytes 1048576 | tf_op jit(solution)/shard_map/all_to_all | solution.py:583
  128.6 19.8 %copy-start.13 = (bf16[128,128]{1,0:T(8,128)(2,1)}, bf16[128,128]{1,0:T(8,128)(2,1)S(1)}, u32[]{:S(2)}) copy-start(bf16[128,128]{1,0:T(8,128)(2,1)S(1)} %collective-permute-done.4.cl_ref) | copy-start | bytes 98308
  128.6 18.1 %collective-permute-start.6 = (bf16[1056,128]{1,0:T(8,128)(2,1)S(1)}, bf16[1056,128]{1,0:T(8,128)(2,1)S(1)}, u32[]{:S(2)}, u32[]{:S(2)}) collective-permute-start(bf16[1056,128]{1,0:T(8,128)(2,1)S(1)} %maximum_dynamic-update-slice_fusion.2), channel_id=1, source_target_pairs={{0,4},{4,8},{8,12},{12,16},{16,20},{20,24},{24,28},{28,32},{32,36}... | collective-permute-start | bytes 811016 | tf_op jit(solution)/shard_map/ppermute | solution.py:510
  130.1 18.3 %collective-permute-start.7 = (bf16[1056,128]{1,0:T(8,128)(2,1)S(1)}, bf16[1056,128]{1,0:T(8,128)(2,1)S(1)}, u32[]{:S(2)}, u32[]{:S(2)}) collective-permute-start(bf16[1056,128]{1,0:T(8,128)(2,1)S(1)} %maximum_dynamic-update-slice_fusion.3), channel_id=1, source_target_pairs={{0,124},{4,0},{8,4},{12,8},{16,12},{20,16},{24,20},{28,24},{32,28}... | collective-permute-start | bytes 811016 | tf_op jit(solution)/shard_map/ppermute | solution.py:510
  146.7 1.6 copy-start.6
  148.4 0.7 copy-start.7
  159.1 0.8 copy-start.2
  (1 other events, 0.7 us)

commit v3 on v2

--- a/solution.py
+++ b/solution.py
@@ -570,10 +570,10 @@
     )
     turned = lax.ppermute(pooled, ("wide", "narrow"), turns(0))
     ends = lax.ppermute(pooled, ("wide", "narrow"), turns(1))
-    slabs = jnp.stack([turned, ends]).reshape(2, 32, 16, 128)
-    slabs = jnp.pad(slabs, ((0, 0), (1, 1), (0, 0), (0, 0)))
-    parcels = jnp.stack([slabs[:, j : j + 32] for j in range(3)], axis=2).transpose(1, 0, 2, 3, 4)
-    got = lax.all_to_all(parcels.reshape(32, 96, 128), "wide", 0, 0, tiled=True)
+    none = jnp.zeros((1, 16, 128), BF)
+    slabs = [jnp.concatenate([none, tile.reshape(32, 16, 128), none]) for tile in (turned, ends)]
+    parcels = jnp.concatenate([padded[j : j + 32] for padded in slabs for j in range(3)], axis=1)
+    got = lax.all_to_all(parcels, "wide", 0, 0, tiled=True)
     near_part = conv1a(at, slab, mate, wa, b_coarse1[None], "near")
     hleft = shift(hcols, "narrow", 1)
     hright = shift(hcols, "narrow", -1)

time: 166 us -> 167 us (level)
  waiting for transfers between devices: 38 us -> 30.8 us
  starting transfers between devices: 52.4 us -> 58.2 us
  local copies, waits for them, and re-layouts: 5.77 us -> 8.95 us
    ppermute x10, waiting for transfers between devices: 23.7 us -> 16.9 us  [shift(): lax.ppermute(array, axis, [(i, (i + by) % count) for i in range(count)])]
    all_to_all x1, starting transfers between devices: 11 us -> 17.1 us  [local(): got = lax.all_to_all(parcels, 'wide', 0, 0, tiled=True)]
    ppermute x1, waiting for transfers between devices: 5.71 us -> 11.5 us  [local(): far = lax.ppermute(mate, 'wide', [(i, j % 32) for i, j in hops])]
    ppermute x1, waiting for transfers between devices: 4.78 us -> 0.01 us  [local(): mate = lax.ppermute(slab, 'wide', [(i, i ^ 1) for i in range(32)])]
    unnamed x34 -> x39, local copies, waits for them, and re-layouts: 4 us -> 7.58 us
    all_to_all x1, starting transfers between devices: 7.99 us -> 4.9 us  [local(): lax.all_to_all(context.reshape(128, 16, 128), ('wide', 'narrow'), 0, 0, t...]
    ppermute x1, starting transfers between devices: 2.75 us -> 5.33 us  [local(): turned = lax.ppermute(pooled, ('wide', 'narrow'), turns(0))]
    ppermute x1, waiting for transfers between devices: 2.01 us -> 0.01 us  [local(): turned = lax.ppermute(pooled, ('wide', 'narrow'), turns(0))]
  transfers between devices with their start and end apart: 16 -> 16, of which waited for: 9 -> 5; matrix products, arithmetic and copies ran while one was open for 2% -> 4% of each run, Pallas kernels for 27% -> 33%
where the time goes in v3:
time: 167 us
  Pallas kernels  66.6 us (40%)
  starting transfers between devices  58.2 us (35%)
  waiting for transfers between devices  30.8 us (18%)
  local copies, waits for them, and re-layouts  8.95 us (5%)
    ppermute x10, starting transfers between devices, shift(): lax.ppermute(array, axis, [(i, (i + by) % count) for i in range(count)])  25.1 us
    all_to_all x1, starting transfers between devices, local(): got = lax.all_to_all(parcels, 'wide', 0, 0, tiled=True)  17.1 us
    ppermute x10, waiting for transfers between devices, shift(): lax.ppermute(array, axis, [(i, (i + by) % count) for i in range(count)])  16.9 us
    pallas_call x2, Pallas kernels, conv1a(): pl.pallas_call(functools.partial(conv1a_body, name == 'distant'), in_spec...  15.4 us
    pallas_call x1, Pallas kernels, coarse(): pl.pallas_call(coarse_body, grid_spec=pltpu.PrefetchScalarGridSpec(num_sc...  13.9 us
    ppermute x1, waiting for transfers between devices, local(): far = lax.ppermute(mate, 'wide', [(i, j % 32) for i, j in hops])  11.5 us
    pallas_call x1, Pallas kernels, fine1(): pl.pallas_call(fine1_body, in_specs=[pl.BlockSpec(memory_space=pltpu.SMEM...  10.6 us
    pallas_call x1, Pallas kernels, fine2(): pl.pallas_call(fine2_body, in_specs=[pl.BlockSpec(memory_space=pltpu.SMEM...  9.97 us
  transfers between devices with their start and end apart: 16, of which 5 were waited for; matrix products, arithmetic and copies ran while one was open for 4% of the time, Pallas kernels for 33%

profile of v3, /device:TPU:1, one launch (start us, length us, event | category | flops | bytes accessed | tf_op | source)
XLA Modules:
  0.0 166.8 jit_solution(11429060493590691562)
XLA Ops:
  0.6 6.2 %prep.1 = (bf16[64,128,128]{2,1,0:T(8,128)(2,1)}, bf16[1056,128]{1,0:T(8,128)(2,1)}, bf16[1056,128]{1,0:T(8,128)(2,1)}, bf16[128,128]{1,0:T(8,128)(2,1)}) custom-call(bf16[16,64,8,128]{3,2,1,0:T(8,128)(2,1)} %x_ref.2), custom_call_target="tpu_custom_call" | custom-call | tf_op jit(solution)/shard_map/prep/pallas_call | solution.py:70
  6.9 1.4 collective-permute-start.1
  8.3 3.0 %collective-permute-start = (bf16[128,128]{1,0:T(8,128)(2,1)}, bf16[128,128]{1,0:T(8,128)(2,1)S(1)}, u32[]{:S(2)}, u32[]{:S(2)}) collective-permute-start(bf16[128,128]{1,0:T(8,128)(2,1)} %get-tuple-element.23), channel_id=1, source_target_pairs={{0,1},{1,2},{2,3},{3,0},{4,5},{5,6},{6,7},{7,4},{8,9},{9,10},{10,1... | collective-permute-start | bytes 98312 | tf_op jit(solution)/shard_map/ppermute | solution.py:510
  11.3 2.2 %cprep.1 = (bf16[2,16,64,128]{3,2,1,0:T(8,128)(2,1)}, bf16[256,128]{1,0:T(8,128)(2,1)}, bf16[256,128]{1,0:T(8,128)(2,1)}) custom-call(bf16[64,2,16,128]{3,2,1,0:T(8,128)(2,1)} %x_ref.3), custom_call_target="tpu_custom_call" | custom-call | tf_op jit(solution)/shard_map/cprep/pallas_call | solution.py:112
  14.1 1.0 collective-permute-start.2
  15.7 5.7 %collective-permute-start.3 = (bf16[1056,128]{1,0:T(8,128)(2,1)}, bf16[1056,128]{1,0:T(8,128)(2,1)S(1)}, u32[]{:S(2)}, u32[]{:S(2)}) collective-permute-start(bf16[1056,128]{1,0:T(8,128)(2,1)} %maximum_dynamic-update-slice_fusion.1), channel_id=1, source_target_pairs={{0,124},{4,0},{8,4},{12,8},{16,12},{20,16},{24,20},{28,24},{32,28}... | collective-permute-start | bytes 811016 | tf_op jit(solution)/shard_map/ppermute | solution.py:510
  21.4 4.1 %collective-permute-start.10 = (bf16[256,128]{1,0:T(8,128)(2,1)}, bf16[256,128]{1,0:T(8,128)(2,1)S(1)}, u32[]{:S(2)}, u32[]{:S(2)}) collective-permute-start(bf16[256,128]{1,0:T(8,128)(2,1)} %get-tuple-element.32), channel_id=1, source_target_pairs={{0,1},{1,2},{2,3},{3,0},{4,5},{5,6},{6,7},{7,4},{8,9},{9,10},{10,1... | collective-permute-start | bytes 196616 | tf_op jit(solution)/shard_map/ppermute | solution.py:510
  25.5 3.2 %weights.1 = (bf16[128,1536]{1,0:T(8,128)(2,1)}, bf16[128,1536]{1,0:T(8,128)(2,1)}, bf16[64,1728]{1,0:T(8,128)(2,1)}, bf16[64,432]{1,0:T(8,128)(2,1)}, bf16[64,1728]{1,0:T(8,128)(2,1)}) custom-call(bf16[27,16,16]{2,1,0:T(8,128)(2,1)} %bitcast.42, bf16[27,16,16]{2,1,0:T(8,128)(2,1)} %bitcast.43, bf16[27,64,80]{2,1,0:T(8,128)(2,1)} %bitcast.38, ...), custom_call_target="tpu_custom_call" | custom-call | tf_op jit(solution)/shard_map/weights/pallas_call | solution.py:146
  30.2 10.6 %fine1.1 = (bf16[64,128,128]{2,1,0:T(8,128)(2,1)}, bf16[512,128]{1,0:T(8,128)(2,1)}, bf16[128,128]{1,0:T(8,128)(2,1)}, bf16[1056,128]{1,0:T(8,128)(2,1)}, bf16[1056,128]{1,0:T(8,128)(2,1)}) custom-call(s32[6]{0:T(128)} %stack.31.at_ref, bf16[64,128,128]{2,1,0:T(8,128)(2,1)} %get-tuple-element.21.x_ref, bf16[1056,128]{1,0:T(8,128)(2,1)} %copy-done.8, ...), custom_call_target="tpu_custom_call" | custom-call | tf_op jit(solution)/shard_map/fine1/pallas_call | solution.py:271
  40.7 5.3 %collective-permute-start.8 = (bf16[512,128]{1,0:T(8,128)(2,1)}, bf16[512,128]{1,0:T(8,128)(2,1)S(1)}, u32[]{:S(2)}, u32[]{:S(2)}) collective-permute-start(bf16[512,128]{1,0:T(8,128)(2,1)} %get-tuple-element.31), channel_id=1, source_target_pairs={{0,0},{1,32},{2,64},{3,96},{4,4},{5,36},{6,68},{7,100},{8,8},{9,40... | collective-permute-start | bytes 393224 | tf_op jit(solution)/shard_map/ppermute | solution.py:571
  46.2 1.1 collective-permute-start.12
  47.3 3.5 %collective-permute-start.9 = (bf16[512,128]{1,0:T(8,128)(2,1)}, bf16[512,128]{1,0:T(8,128)(2,1)S(1)}, u32[]{:S(2)}, u32[]{:S(2)}) collective-permute-start(bf16[512,128]{1,0:T(8,128)(2,1)} %get-tuple-element.31), channel_id=1, source_target_pairs={{0,3},{1,35},{2,67},{3,99},{4,4},{5,36},{6,68},{7,100},{8,8},{9,40... | collective-permute-start | bytes 393224 | tf_op jit(solution)/shard_map/ppermute | solution.py:572
  53.0 2.4 %collective-permute-done.9 = bf16[512,128]{1,0:T(8,128)(2,1)S(1)} collective-permute-done((bf16[512,128]{1,0:T(8,128)(2,1)}, bf16[512,128]{1,0:T(8,128)(2,1)S(1)}, u32[]{:S(2)}, u32[]{:S(2)}) %collective-permute-start.9) | collective-permute-done | bytes 131104 | tf_op jit(solution)/shard_map/ppermute | solution.py:572
  57.5 17.1 %all-to-all-start = ((bf16[32,96,128]{2,1,0:T(8,128)(2,1)}), bf16[32,96,128]{2,1,0:T(8,128)(2,1)S(1)}, u32[]{:S(2)}, u32[]{:S(2)}) async-start(bf16[32,96,128]{2,1,0:T(8,128)(2,1)} %fusion.3), calls=%async_computation | async-start | bytes 1572864 | tf_op jit(solution)/shard_map/all_to_all | solution.py:576
  74.6 1.3 collective-permute-start.13
  75.9 1.9 %collective-permute-start.5 = (bf16[128,128]{1,0:T(8,128)(2,1)S(1)}, bf16[128,128]{1,0:T(8,128)(2,1)S(1)}, u32[]{:S(2)}, u32[]{:S(2)}) collective-permute-start(bf16[128,128]{1,0:T(8,128)(2,1)S(1)} %copy-done.16), channel_id=1, source_target_pairs={{0,3},{1,0},{2,1},{3,2},{4,7},{5,4},{6,5},{7,6},{8,11},{9,8},{10,9... | collective-permute-start | bytes 98312 | tf_op jit(solution)/shard_map/ppermute | solution.py:510
  77.8 1.3 collective-permute-start.4
  79.1 3.7 %collective-permute-done.5.cr_ref = bf16[128,128]{1,0:T(8,128)(2,1)S(1)} collective-permute-done((bf16[128,128]{1,0:T(8,128)(2,1)S(1)}, bf16[128,128]{1,0:T(8,128)(2,1)S(1)}, u32[]{:S(2)}, u32[]{:S(2)}) %collective-permute-start.5) | collective-permute-done | bytes 32800 | tf_op jit(solution)/shard_map/ppermute | solution.py:510
  82.8 7.7 %shard_map.122.near_ref = f32[18,64,256]{2,1,0:T(8,128)} custom-call(s32[6]{0:T(128)} %stack.31.at_ref, bf16[2,20,64,128]{3,2,1,0:T(8,128)(2,1)} %copy-done, bf16[2,20,64,128]{3,2,1,0:T(8,128)(2,1)} %copy-done.3, bf16[64,1728]{1,0:T(8,128)(2,1)} %get-tuple-element.35.w_ref, f32[1,64]{1,0:T(1,128)} %bitcast.44), custom_call_target="tpu_custom_call" | custom-call | tf_op jit(solution)/shard_map/pallas_call | solution.py:394
  90.5 11.5 %collective-permute-done.13.first_ref = bf16[2,20,64,128]{3,2,1,0:T(8,128)(2,1)S(1)} collective-permute-done((bf16[2,20,64,128]{3,2,1,0:T(8,128)(2,1)S(1)}, bf16[2,20,64,128]{3,2,1,0:T(8,128)(2,1)S(1)}, u32[]{:S(2)}, u32[]{:S(2)}) %collective-permute-start.13) | collective-permute-done | bytes 655392 | tf_op jit(solution)/shard_map/ppermute | solution.py:567
  102.0 0.9 copy-done.4
  102.9 7.7 %shard_map.123.far_ref = f32[18,64,256]{2,1,0:T(8,128)} custom-call(s32[6]{0:T(128)} %stack.31.at_ref, bf16[2,20,64,128]{3,2,1,0:T(8,128)(2,1)} %copy-done.4, bf16[2,20,64,128]{3,2,1,0:T(8,128)(2,1)} %copy-done, bf16[64,1728]{1,0:T(8,128)(2,1)} %get-tuple-element.35.w_ref, f32[1,64]{1,0:T(1,128)} %bitcast.45), custom_call_target="tpu_custom_call" | custom-call | tf_op jit(solution)/shard_map/pallas_call | solution.py:394
  110.6 0.9 copy-done.1
  111.4 13.9 %coarse.1 = (bf16[64,2,16,128]{3,2,1,0:T(8,128)(2,1)}, bf16[4,8,4,16,128]{4,3,2,1,0:T(8,128)(2,1)}) custom-call(s32[6]{0:T(128)} %stack.31.at_ref, bf16[32,2,48,128]{3,2,1,0:T(8,128)(2,1)} %bitcast.29, f32[18,64,256]{2,1,0:T(8,128)} %shard_map.122.near_ref, f32[18,64,256]{2,1,0:T(8,128)} %shard_map.123.far_ref, bf16[64,432]{1,0:T(8,128)(2,1)} %get-tuple-element.36.w1_ref, ...), custom_call_target="tpu_custom_call" | custom-call | tf_op jit(solution)/shard_map/coarse/pallas_call | solution.py:477
  125.3 4.9 %all-to-all-start.1 = ((bf16[128,16,128]{2,1,0:T(8,128)(2,1)}), bf16[128,16,128]{2,1,0:T(8,128)(2,1)S(1)}, u32[]{:S(2)}, u32[]{:S(2)}) async-start(bf16[128,16,128]{2,1,0:T(8,128)(2,1)} %bitcast.37), calls=%async_computation.1 | async-start | bytes 1048576 | tf_op jit(solution)/shard_map/all_to_all | solution.py:583
  130.3 1.4 collective-permute-start.6
  131.7 5.2 %collective-permute-start.7 = (bf16[1056,128]{1,0:T(8,128)(2,1)S(1)}, bf16[1056,128]{1,0:T(8,128)(2,1)S(1)}, u32[]{:S(2)}, u32[]{:S(2)}) collective-permute-start(bf16[1056,128]{1,0:T(8,128)(2,1)S(1)} %maximum_dynamic-update-slice_fusion.3), channel_id=1, source_target_pairs={{0,124},{4,0},{8,4},{12,8},{16,12},{20,16},{24,20},{28,24},{32,28}... | collective-permute-start | bytes 811016 | tf_op jit(solution)/shard_map/ppermute | solution.py:510
  136.9 11.6 %collective-permute-done.6.top_ref = bf16[1056,128]{1,0:T(8,128)(2,1)S(1)} collective-permute-done((bf16[1056,128]{1,0:T(8,128)(2,1)S(1)}, bf16[1056,128]{1,0:T(8,128)(2,1)S(1)}, u32[]{:S(2)}, u32[]{:S(2)}) %collective-permute-start.6) | collective-permute-done | bytes 270368 | tf_op jit(solution)/shard_map/ppermute | solution.py:510
  148.4 1.6 collective-permute-done.7.bot_ref
  150.8 10.0 %fine2.1.t_ref = bf16[64,128,128]{2,1,0:T(8,128)(2,1)} custom-call(s32[6]{0:T(128)} %stack.31.at_ref, bf16[64,128,128]{2,1,0:T(8,128)(2,1)} %get-tuple-element.26.x_ref, bf16[1056,128]{1,0:T(8,128)(2,1)} %copy-done.6, bf16[1056,128]{1,0:T(8,128)(2,1)} %copy-done.7, bf16[128,128]{1,0:T(8,128)(2,1)} %copy-done.13, bf16[128,128]{1,0:T(8,128)(2,1)} %copy-done.12, ...), custom_call_target="tpu_custom_call" | custom-call | tf_op jit(solution)/shard_map/fine2/pallas_call | solution.py:301
  160.8 0.8 copy-done.2
  161.5 5.2 %final.1 = bf16[16,64,8,128]{3,2,1,0:T(8,128)(2,1)} custom-call(s32[6]{0:T(128)} %stack.31.at_ref, bf16[64,128,128]{2,1,0:T(8,128)(2,1)} %fine2.1.t_ref, bf16[32,4,16,128]{3,2,1,0:T(8,128)(2,1)} %bitcast.30), custom_call_target="tpu_custom_call" | custom-call | tf_op jit(solution)/shard_map/final/pallas_call | solution.py:332
  (61 shorter events, 7.7 us)
Async XLA Ops:
  6.9 6.6 %collective-permute-start.1 = (bf16[128,128]{1,0:T(8,128)(2,1)}, bf16[128,128]{1,0:T(8,128)(2,1)S(1)}, u32[]{:S(2)}, u32[]{:S(2)}) collective-permute-start(bf16[128,128]{1,0:T(8,128)(2,1)} %get-tuple-element.23), channel_id=1, source_target_pairs={{0,3},{1,0},{2,1},{3,2},{4,7},{5,4},{6,5},{7,6},{8,11},{9,8},{10,9... | collective-permute-start | bytes 98312 | tf_op jit(solution)/shard_map/ppermute | solution.py:510
  8.3 5.2 %collective-permute-start = (bf16[128,128]{1,0:T(8,128)(2,1)}, bf16[128,128]{1,0:T(8,128)(2,1)S(1)}, u32[]{:S(2)}, u32[]{:S(2)}) collective-permute-start(bf16[128,128]{1,0:T(8,128)(2,1)} %get-tuple-element.23), channel_id=1, source_target_pairs={{0,1},{1,2},{2,3},{3,0},{4,5},{5,6},{6,7},{7,4},{8,9},{9,10},{10,1... | collective-permute-start | bytes 98312 | tf_op jit(solution)/shard_map/ppermute | solution.py:510
  13.5 15.9 %collective-permute-start.11 = (bf16[256,128]{1,0:T(8,128)(2,1)}, bf16[256,128]{1,0:T(8,128)(2,1)S(1)}, u32[]{:S(2)}, u32[]{:S(2)}) collective-permute-start(bf16[256,128]{1,0:T(8,128)(2,1)} %get-tuple-element.34), channel_id=1, source_target_pairs={{0,3},{1,0},{2,1},{3,2},{4,7},{5,4},{6,5},{7,6},{8,11},{9,8},{10,9... | collective-permute-start | bytes 196616 | tf_op jit(solution)/shard_map/ppermute | solution.py:510
  13.5 15.9 %copy-start.10 = (bf16[128,128]{1,0:T(8,128)(2,1)}, bf16[128,128]{1,0:T(8,128)(2,1)S(1)}, u32[]{:S(2)}) copy-start(bf16[128,128]{1,0:T(8,128)(2,1)S(1)} %collective-permute-done.1.cr_ref) | copy-start | bytes 98308
  13.5 15.9 %copy-start.11 = (bf16[128,128]{1,0:T(8,128)(2,1)}, bf16[128,128]{1,0:T(8,128)(2,1)S(1)}, u32[]{:S(2)}) copy-start(bf16[128,128]{1,0:T(8,128)(2,1)S(1)} %collective-permute-done.cl_ref) | copy-start | bytes 98308
  14.1 15.2 %collective-permute-start.2 = (bf16[1056,128]{1,0:T(8,128)(2,1)}, bf16[1056,128]{1,0:T(8,128)(2,1)S(1)}, u32[]{:S(2)}, u32[]{:S(2)}) collective-permute-start(bf16[1056,128]{1,0:T(8,128)(2,1)} %maximum_dynamic-update-slice_fusion), channel_id=1, source_target_pairs={{0,4},{4,8},{8,12},{12,16},{16,20},{20,24},{24,28},{28,32},{32,36}... | collective-permute-start | bytes 811016 | tf_op jit(solution)/shard_map/ppermute | solution.py:510
  15.7 13.7 %collective-permute-start.3 = (bf16[1056,128]{1,0:T(8,128)(2,1)}, bf16[1056,128]{1,0:T(8,128)(2,1)S(1)}, u32[]{:S(2)}, u32[]{:S(2)}) collective-permute-start(bf16[1056,128]{1,0:T(8,128)(2,1)} %maximum_dynamic-update-slice_fusion.1), channel_id=1, source_target_pairs={{0,124},{4,0},{8,4},{12,8},{16,12},{20,16},{24,20},{28,24},{32,28}... | collective-permute-start | bytes 811016 | tf_op jit(solution)/shard_map/ppermute | solution.py:510
  21.4 24.7 %collective-permute-start.10 = (bf16[256,128]{1,0:T(8,128)(2,1)}, bf16[256,128]{1,0:T(8,128)(2,1)S(1)}, u32[]{:S(2)}, u32[]{:S(2)}) collective-permute-start(bf16[256,128]{1,0:T(8,128)(2,1)} %get-tuple-element.32), channel_id=1, source_target_pairs={{0,1},{1,2},{2,3},{3,0},{4,5},{5,6},{6,7},{7,4},{8,9},{9,10},{10,1... | collective-permute-start | bytes 196616 | tf_op jit(solution)/shard_map/ppermute | solution.py:510
  25.5 20.6 %copy-start.5 = (bf16[2,16,64,128]{3,2,1,0:T(8,128)(2,1)S(1)}, bf16[2,16,64,128]{3,2,1,0:T(8,128)(2,1)}, u32[]{:S(2)}) copy-start(bf16[2,16,64,128]{3,2,1,0:T(8,128)(2,1)} %get-tuple-element.33) | copy-start | bytes 1572868
  29.4 0.8 copy-start.9
  40.7 10.1 %collective-permute-start.8 = (bf16[512,128]{1,0:T(8,128)(2,1)}, bf16[512,128]{1,0:T(8,128)(2,1)S(1)}, u32[]{:S(2)}, u32[]{:S(2)}) collective-permute-start(bf16[512,128]{1,0:T(8,128)(2,1)} %get-tuple-element.31), channel_id=1, source_target_pairs={{0,0},{1,32},{2,64},{3,96},{4,4},{5,36},{6,68},{7,100},{8,8},{9,40... | collective-permute-start | bytes 393224 | tf_op jit(solution)/shard_map/ppermute | solution.py:571
  46.1 29.8 %copy-start.16 = (bf16[128,128]{1,0:T(8,128)(2,1)S(1)}, bf16[128,128]{1,0:T(8,128)(2,1)}, u32[]{:S(2)}) copy-start(bf16[128,128]{1,0:T(8,128)(2,1)} %get-tuple-element.28) | copy-start | bytes 98308
  46.2 36.6 %copy-start = (bf16[2,20,64,128]{3,2,1,0:T(8,128)(2,1)}, bf16[2,20,64,128]{3,2,1,0:T(8,128)(2,1)S(1)}, u32[]{:S(2)}) copy-start(bf16[2,20,64,128]{3,2,1,0:T(8,128)(2,1)S(1)} %pad_maximum_fusion.first_ref.second_ref) | copy-start | bytes 1966084
  46.2 28.3 %collective-permute-start.12 = (bf16[2,20,64,128]{3,2,1,0:T(8,128)(2,1)S(1)}, bf16[2,20,64,128]{3,2,1,0:T(8,128)(2,1)S(1)}, u32[]{:S(2)}, u32[]{:S(2)}) collective-permute-start(bf16[2,20,64,128]{3,2,1,0:T(8,128)(2,1)S(1)} %pad_maximum_fusion.first_ref.second_ref), channel_id=1, source_target_pairs={{0,4},{4,0},{8,12},{12,8},{16,20},{20,16},{24,28},{28,24},{32,36},... | collective-permute-start | bytes 1966088 | tf_op jit(solution)/shard_map/ppermute | solution.py:560
  47.3 8.1 %collective-permute-start.9 = (bf16[512,128]{1,0:T(8,128)(2,1)}, bf16[512,128]{1,0:T(8,128)(2,1)S(1)}, u32[]{:S(2)}, u32[]{:S(2)}) collective-permute-start(bf16[512,128]{1,0:T(8,128)(2,1)} %get-tuple-element.31), channel_id=1, source_target_pairs={{0,3},{1,35},{2,67},{3,99},{4,4},{5,36},{6,68},{7,100},{8,8},{9,40... | collective-permute-start | bytes 393224 | tf_op jit(solution)/shard_map/ppermute | solution.py:572
  57.5 53.1 %all-to-all-start = ((bf16[32,96,128]{2,1,0:T(8,128)(2,1)}), bf16[32,96,128]{2,1,0:T(8,128)(2,1)S(1)}, u32[]{:S(2)}, u32[]{:S(2)}) async-start(bf16[32,96,128]{2,1,0:T(8,128)(2,1)} %fusion.3), calls=%async_computation | async-start | bytes 1572864 | tf_op jit(solution)/shard_map/all_to_all | solution.py:576
  74.6 8.2 %copy-start.3 = (bf16[2,20,64,128]{3,2,1,0:T(8,128)(2,1)}, bf16[2,20,64,128]{3,2,1,0:T(8,128)(2,1)S(1)}, u32[]{:S(2)}) copy-start(bf16[2,20,64,128]{3,2,1,0:T(8,128)(2,1)S(1)} %collective-permute-done.12.second_ref) | copy-start | bytes 1966084
  74.6 27.4 %collective-permute-start.13 = (bf16[2,20,64,128]{3,2,1,0:T(8,128)(2,1)S(1)}, bf16[2,20,64,128]{3,2,1,0:T(8,128)(2,1)S(1)}, u32[]{:S(2)}, u32[]{:S(2)}) collective-permute-start(bf16[2,20,64,128]{3,2,1,0:T(8,128)(2,1)S(1)} %collective-permute-done.12.second_ref), channel_id=1, source_target_pairs={{0,8},{4,124},{8,16},{12,4},{16,24},{20,12},{24,32},{28,20},{32,40... | collective-permute-start | bytes 1966088 | tf_op jit(solution)/shard_map/ppermute | solution.py:567
  75.9 6.9 %collective-permute-start.5 = (bf16[128,128]{1,0:T(8,128)(2,1)S(1)}, bf16[128,128]{1,0:T(8,128)(2,1)S(1)}, u32[]{:S(2)}, u32[]{:S(2)}) collective-permute-start(bf16[128,128]{1,0:T(8,128)(2,1)S(1)} %copy-done.16), channel_id=1, source_target_pairs={{0,3},{1,0},{2,1},{3,2},{4,7},{5,4},{6,5},{7,6},{8,11},{9,8},{10,9... | collective-permute-start | bytes 98312 | tf_op jit(solution)/shard_map/ppermute | solution.py:510
  77.8 52.4 %collective-permute-start.4 = (bf16[128,128]{1,0:T(8,128)(2,1)S(1)}, bf16[128,128]{1,0:T(8,128)(2,1)S(1)}, u32[]{:S(2)}, u32[]{:S(2)}) collective-permute-start(bf16[128,128]{1,0:T(8,128)(2,1)S(1)} %copy-done.16), channel_id=1, source_target_pairs={{0,1},{1,2},{2,3},{3,0},{4,5},{5,6},{6,7},{7,4},{8,9},{9,10},{10,1... | collective-permute-start | bytes 98312 | tf_op jit(solution)/shard_map/ppermute | solution.py:510
  82.8 27.8 %copy-start.12 = (bf16[128,128]{1,0:T(8,128)(2,1)}, bf16[128,128]{1,0:T(8,128)(2,1)S(1)}, u32[]{:S(2)}) copy-start(bf16[128,128]{1,0:T(8,128)(2,1)S(1)} %collective-permute-done.5.cr_ref) | copy-start | bytes 98308
  102.0 0.9 copy-start.4
  110.6 0.9 copy-start.1
  111.4 18.8 %copy-start.15 = (bf16[1056,128]{1,0:T(8,128)(2,1)S(1)}, bf16[1056,128]{1,0:T(8,128)(2,1)}, u32[]{:S(2)}) copy-start(bf16[1056,128]{1,0:T(8,128)(2,1)} %get-tuple-element.27) | copy-start | bytes 811012
  111.4 20.3 %copy-start.14 = (bf16[1056,128]{1,0:T(8,128)(2,1)S(1)}, bf16[1056,128]{1,0:T(8,128)(2,1)}, u32[]{:S(2)}) copy-start(bf16[1056,128]{1,0:T(8,128)(2,1)} %get-tuple-element.29) | copy-start | bytes 811012
  125.3 35.4 %all-to-all-start.1 = ((bf16[128,16,128]{2,1,0:T(8,128)(2,1)}), bf16[128,16,128]{2,1,0:T(8,128)(2,1)S(1)}, u32[]{:S(2)}, u32[]{:S(2)}) async-start(bf16[128,16,128]{2,1,0:T(8,128)(2,1)} %bitcast.37), calls=%async_computation.1 | async-start | bytes 1048576 | tf_op jit(solution)/shard_map/all_to_all | solution.py:583
  130.2 19.8 %copy-start.13 = (bf16[128,128]{1,0:T(8,128)(2,1)}, bf16[128,128]{1,0:T(8,128)(2,1)S(1)}, u32[]{:S(2)}) copy-start(bf16[128,128]{1,0:T(8,128)(2,1)S(1)} %collective-permute-done.4.cl_ref) | copy-start | bytes 98308
  130.3 18.2 %collective-permute-start.6 = (bf16[1056,128]{1,0:T(8,128)(2,1)S(1)}, bf16[1056,128]{1,0:T(8,128)(2,1)S(1)}, u32[]{:S(2)}, u32[]{:S(2)}) collective-permute-start(bf16[1056,128]{1,0:T(8,128)(2,1)S(1)} %maximum_dynamic-update-slice_fusion.2), channel_id=1, source_target_pairs={{0,4},{4,8},{8,12},{12,16},{16,20},{20,24},{24,28},{28,32},{32,36}... | collective-permute-start | bytes 811016 | tf_op jit(solution)/shard_map/ppermute | solution.py:510
  131.7 18.4 %collective-permute-start.7 = (bf16[1056,128]{1,0:T(8,128)(2,1)S(1)}, bf16[1056,128]{1,0:T(8,128)(2,1)S(1)}, u32[]{:S(2)}, u32[]{:S(2)}) collective-permute-start(bf16[1056,128]{1,0:T(8,128)(2,1)S(1)} %maximum_dynamic-update-slice_fusion.3), channel_id=1, source_target_pairs={{0,124},{4,0},{8,4},{12,8},{16,12},{20,16},{24,20},{28,24},{32,28}... | collective-permute-start | bytes 811016 | tf_op jit(solution)/shard_map/ppermute | solution.py:510
  148.4 1.6 copy-start.6
  150.1 0.7 copy-start.7
  160.8 0.8 copy-start.2
  (1 other events, 0.7 us)
